TPU v7x, 32 devices: a whole 2x2x4 slice. The times are simulated.
32 devices in a mesh: dp: 8 (over z, x), tensor: 4 (over y, core).
Axes of the slice: x: 2, y: 2, z: 4, core: 2. Of those that a mesh axis runs over, the one named last changes fastest.
Arguments:
- tokens: bfloat16 [16384, 768], P(('dp', 'tensor')), may hold values from -6 to 6
- stack: bfloat16 [4, 16384, 768], P(None, ('dp', 'tensor')), may hold values from -6 to 6
- cotangent: bfloat16 [16384, 768], P(('dp', 'tensor')), may hold values from -6 to 6
- starts: int32 [16, 2], P('dp'), may hold values from 0 to 768
- w_query: bfloat16 [768, 768], P('dp', 'tensor'), may hold values from -0.21875 to 0.21875
- w_key: bfloat16 [768, 768], P('dp', 'tensor'), may hold values from -0.21875 to 0.21875
- w_value: bfloat16 [768, 768], P('dp', 'tensor'), may hold values from -0.21875 to 0.21875
- w_output: bfloat16 [768, 768], P('tensor', 'dp'), may hold values from -0.875 to 0.875
- w_in: bfloat16 [768, 3072], P('dp', 'tensor'), may hold values from -0.21875 to 0.21875
- w_out: bfloat16 [3072, 768], P('tensor', 'dp'), may hold values from -0.109375 to 0.109375
- gain_one: float32 [768], replicated, may hold values from 0.1 to 1.9
- shift_one: float32 [768], replicated, may hold values from -3 to 3
- gain_two: float32 [768], replicated, may hold values from 0.1 to 1.9
- shift_two: float32 [768], replicated, may hold values from -3 to 3
- bias_in: float32 [3072], replicated, may hold values from -3 to 3
- bias_out: float32 [768], replicated, may hold values from -3 to 3
- depth_weights: float32 [5], replicated, may hold values from 0.3 to 1.2
Outputs:
- layer_out: bfloat16 [16384, 768], P(('dp', 'tensor'))
- grad_tokens: float32 [16384, 768], P(('dp', 'tensor'))
- grad_stack: float32 [4, 16384, 768], P(None, ('dp', 'tensor'))
- grad_w_query: float32 [768, 768], P('dp', 'tensor')
- grad_w_key: float32 [768, 768], P('dp', 'tensor')
- grad_w_value: float32 [768, 768], P('dp', 'tensor')
- grad_w_output: float32 [768, 768], P('tensor', 'dp')
- grad_w_in: float32 [768, 3072], P('dp', 'tensor')
- grad_w_out: float32 [3072, 768], P('tensor', 'dp')
- grad_gain_one: float32 [768], replicated
- grad_shift_one: float32 [768], replicated
- grad_gain_two: float32 [768], replicated
- grad_shift_two: float32 [768], replicated
- grad_bias_in: float32 [3072], replicated
- grad_bias_out: float32 [768], replicated
- grad_depth: float32 [5], replicated
All inputs are finite; a program needn't handle non-finite values.
Results may differ from a plain program's by a relative error of at most 0.012.
Values may be sent and summed in bfloat16 or wider, within the bound.
A program may use at most 128 MiB of HBM per device.

v0:
```python
import functools
import math

import jax
import jax.numpy as jnp
import numpy as np
from jax import lax
from jax.experimental import pallas as pl
from jax.experimental.pallas import tpu as pltpu
from jax.sharding import PartitionSpec as P

HEAD_DIM = 64
PIECE = 256


EPSILON = 1e-05
NEGATIVE = -1e30


def layer_norm(values, gain, shift):
    centre = values - jnp.mean(values, axis=-1, keepdims=True)
    spread = jnp.mean(centre * centre, axis=-1, keepdims=True)
    return centre * lax.rsqrt(spread + EPSILON) * gain + shift


def tables(seq_length, head_size):
    half_dim = head_size // 2
    frequency = jnp.exp(
        -jnp.log(10000.0) * jnp.arange(half_dim, dtype=jnp.float32) * 2.0 / head_size
    )
    angles = jnp.arange(seq_length, dtype=jnp.float32)[:, None] * frequency[None, :]
    return (jnp.cos(angles), jnp.sin(angles))


def rotate(values, cosine_table, sine_table):
    half_dim = values.shape[-1] // 2
    front_half = values[..., :half_dim]
    back_half = values[..., half_dim:]
    cosines = cosine_table[:, None, :]
    sine_rows = sine_table[:, None, :]
    return jnp.concatenate(
        [
            front_half * cosines - back_half * sine_rows,
            back_half * cosines + front_half * sine_rows,
        ],
        axis=-1,
    )


def allowed_mask(starts, seq_length, piece_size):
    position = jnp.arange(seq_length, dtype=jnp.int32)
    inside = (position[None, None, :] >= starts[:, :, None]) & (
        position[None, None, :] < starts[:, :, None] + piece_size
    )
    jointly = jnp.any(inside[:, :, :, None] & inside[:, :, None, :], axis=1)
    return jointly | (position[None, :, None] >= position[None, None, :])


def gelu_tanh(values):
    return jax.nn.gelu(values, approximate=True)


def right_transposed(matrix, weight):
    return lax.dot_general(
        matrix, weight, (((1,), (1,)), ((), ())), preferred_element_type=jnp.float32
    )


def left_transposed(matrix, other):
    return lax.dot_general(
        matrix, other, (((0,), (0,)), ((), ())), preferred_element_type=jnp.float32
    )


def attend_forward(query, key_rows, value_rows, allowed, score_scale):

    def one_sequence(entries):
        query_seq, key_seq, value_seq, allowed_seq = entries
        scores = (
            jnp.einsum("qhd,khd->hqk", query_seq, key_seq, preferred_element_type=jnp.float32)
            * score_scale
        )
        scores = jnp.where(allowed_seq[None], scores, NEGATIVE)
        highest = jnp.max(scores, axis=-1, keepdims=True)
        powers = jnp.exp(scores - highest)
        row_total = jnp.sum(powers, axis=-1, keepdims=True)
        attention = (powers / row_total).astype(jnp.bfloat16)
        mixed_rows = jnp.einsum(
            "hqk,khd->qhd", attention, value_seq, preferred_element_type=jnp.float32
        )
        return (mixed_rows.astype(jnp.bfloat16), highest + jnp.log(row_total))

    return lax.map(one_sequence, (query, key_rows, value_rows, allowed))


def attend_backward(query, key_rows, value_rows, grad_mixed, log_totals, allowed, score_scale):

    def one_sequence(entries):
        query_seq, key_seq, value_seq, grad_seq, log_seq, allowed_seq = entries
        scores = (
            jnp.einsum("qhd,khd->hqk", query_seq, key_seq, preferred_element_type=jnp.float32)
            * score_scale
        )
        scores = jnp.where(allowed_seq[None], scores, NEGATIVE)
        attention = jnp.exp(scores - log_seq)
        grad_value = jnp.einsum(
            "hqk,qhd->khd",
            attention.astype(jnp.bfloat16),
            grad_seq,
            preferred_element_type=jnp.float32,
        )
        grad_attention = jnp.einsum(
            "qhd,khd->hqk", grad_seq, value_seq, preferred_element_type=jnp.float32
        )
        row_delta = jnp.sum(attention * grad_attention, axis=-1, keepdims=True)
        grad_scores = (attention * (grad_attention - row_delta)).astype(jnp.bfloat16)
        grad_query = (
            jnp.einsum("hqk,khd->qhd", grad_scores, key_seq, preferred_element_type=jnp.float32)
            * score_scale
        )
        grad_key = (
            jnp.einsum("hqk,qhd->khd", grad_scores, query_seq, preferred_element_type=jnp.float32)
            * score_scale
        )
        return (grad_query, grad_key, grad_value.astype(jnp.bfloat16))

    return lax.map(one_sequence, (query, key_rows, value_rows, grad_mixed, log_totals, allowed))


def plain_device(
    tokens,
    stack,
    cotangent,
    starts,
    w_query,
    w_key,
    w_value,
    w_output,
    w_in,
    w_out,
    gain_one,
    shift_one,
    gain_two,
    shift_two,
    bias_in,
    bias_out,
    depth_weights,
):
    rows_here = tokens.shape[0]
    features = tokens.shape[1]
    groups = lax.axis_size("tensor")
    position = lax.axis_index("tensor")
    seq_count = starts.shape[0]
    seq_length = rows_here * groups // seq_count
    score_scale = 1.0 / math.sqrt(HEAD_DIM)
    local_heads = w_query.shape[1] // HEAD_DIM
    hidden = w_in.shape[1]
    cosine_table, sine_table = tables(seq_length, HEAD_DIM)
    allowed = allowed_mask(starts, seq_length, PIECE)

    def to_heads(matrix):
        return matrix.reshape(seq_count, seq_length, local_heads, HEAD_DIM)

    def from_heads(blocks):
        return blocks.reshape(seq_count * seq_length, local_heads * HEAD_DIM)

    def share_rows(local_rows):
        return lax.all_gather(local_rows, "tensor", axis=0, tiled=True)

    def share_grad(local_rows):
        return lax.all_gather(local_rows, "tensor", axis=0, tiled=True)

    def merge_rows(source, weight):
        return lax.psum_scatter(
            jnp.dot(source, weight, preferred_element_type=jnp.float32),
            "tensor",
            scatter_dimension=0,
            tiled=True,
        )

    def return_rows(pairs):
        running = jnp.zeros((lax.axis_size("tensor") * rows_here, features), jnp.float32)
        for source, weight in pairs:
            running = running + right_transposed(source, weight)
        return lax.psum_scatter(running, "tensor", scatter_dimension=0, tiled=True)

    query_w, key_w, value_w, output_w = (
        lax.all_gather(w_query, "dp", axis=0, tiled=True),
        lax.all_gather(w_key, "dp", axis=0, tiled=True),
        lax.all_gather(w_value, "dp", axis=0, tiled=True),
        lax.all_gather(w_output, "dp", axis=1, tiled=True),
    )
    inner_w, outer_w = (
        lax.all_gather(w_in, "dp", axis=0, tiled=True),
        lax.all_gather(w_out, "dp", axis=1, tiled=True),
    )
    token_rows = tokens.astype(jnp.float32)
    normed_one = layer_norm(token_rows, gain_one, shift_one).astype(jnp.bfloat16)
    normed_all = share_rows(normed_one)
    query = rotate(
        to_heads(jnp.dot(normed_all, query_w, preferred_element_type=jnp.float32)),
        cosine_table,
        sine_table,
    ).astype(jnp.bfloat16)
    key_rows = rotate(
        to_heads(jnp.dot(normed_all, key_w, preferred_element_type=jnp.float32)),
        cosine_table,
        sine_table,
    ).astype(jnp.bfloat16)
    value_rows = to_heads(jnp.dot(normed_all, value_w, preferred_element_type=jnp.float32)).astype(
        jnp.bfloat16
    )
    mixed_heads, log_totals = attend_forward(query, key_rows, value_rows, allowed, score_scale)
    mixed_flat = from_heads(mixed_heads)
    middle = token_rows + merge_rows(mixed_flat, output_w)
    normed_two = layer_norm(middle, gain_two, shift_two).astype(jnp.bfloat16)
    second_all = share_rows(normed_two)
    bias_slice = lax.dynamic_slice_in_dim(bias_in, position * hidden, hidden)
    pre_act = jnp.dot(second_all, inner_w, preferred_element_type=jnp.float32) + bias_slice
    activated = gelu_tanh(pre_act).astype(jnp.bfloat16)
    block_out = middle + merge_rows(activated, outer_w) + bias_out
    averaged = depth_weights[4] * block_out
    for layer_index in range(4):
        averaged = averaged + depth_weights[layer_index] * stack[layer_index].astype(jnp.float32)
    layer_out = averaged.astype(jnp.bfloat16)
    grad_rows = cotangent.astype(jnp.float32)
    grad_stack = jnp.stack([depth_weights[layer_index] * grad_rows for layer_index in range(4)])
    depth_terms = jnp.stack(
        [jnp.sum(stack[layer_index].astype(jnp.float32) * grad_rows) for layer_index in range(4)]
        + [jnp.sum(block_out * grad_rows)]
    )
    grad_block = depth_weights[4] * grad_rows
    grad_bias_out = jnp.sum(grad_block, axis=0)
    grad_sent = share_grad(grad_block.astype(jnp.bfloat16))
    grad_outer = left_transposed(activated, grad_sent)
    grad_act = right_transposed(grad_sent, outer_w)
    grad_pre = jax.vjp(gelu_tanh, pre_act)[1](grad_act)[0].astype(jnp.bfloat16)
    grad_bias_slice = jnp.sum(grad_pre.astype(jnp.float32), axis=0)
    bias_full = lax.dynamic_update_slice_in_dim(
        jnp.zeros((bias_in.shape[0],), jnp.float32), grad_bias_slice, position * hidden, 0
    )
    grad_inner = left_transposed(second_all, grad_pre)
    grad_norm_two = return_rows(((grad_pre, inner_w),))
    layer_two = jax.vjp(layer_norm, middle, gain_two, shift_two)[1](grad_norm_two)
    grad_middle = grad_block + layer_two[0]
    grad_attn_sent = share_grad(grad_middle.astype(jnp.bfloat16))
    grad_output_w = left_transposed(mixed_flat, grad_attn_sent)
    grad_mixed = right_transposed(grad_attn_sent, output_w).astype(jnp.bfloat16)
    grad_query, grad_key, grad_value = attend_backward(
        query, key_rows, value_rows, to_heads(grad_mixed), log_totals, allowed, score_scale
    )
    grad_query = from_heads(rotate(grad_query, cosine_table, -sine_table)).astype(jnp.bfloat16)
    grad_key = from_heads(rotate(grad_key, cosine_table, -sine_table)).astype(jnp.bfloat16)
    grad_value = from_heads(grad_value)
    grad_query_w = left_transposed(normed_all, grad_query)
    grad_key_w = left_transposed(normed_all, grad_key)
    grad_value_w = left_transposed(normed_all, grad_value)
    grad_norm_one = return_rows(((grad_query, query_w), (grad_key, key_w), (grad_value, value_w)))
    layer_one = jax.vjp(layer_norm, token_rows, gain_one, shift_one)[1](grad_norm_one)
    grad_tokens = grad_middle + layer_one[0]
    grad_w_query, grad_w_key, grad_w_value, grad_w_output, grad_w_in, grad_w_out = (
        lax.psum_scatter(grad_query_w, "dp", scatter_dimension=0, tiled=True),
        lax.psum_scatter(grad_key_w, "dp", scatter_dimension=0, tiled=True),
        lax.psum_scatter(grad_value_w, "dp", scatter_dimension=0, tiled=True),
        lax.psum_scatter(grad_output_w, "dp", scatter_dimension=1, tiled=True),
        lax.psum_scatter(grad_inner, "dp", scatter_dimension=0, tiled=True),
        lax.psum_scatter(grad_outer, "dp", scatter_dimension=1, tiled=True),
    )
    summed = lax.psum(
        (
            layer_one[1],
            layer_one[2],
            layer_two[1],
            layer_two[2],
            bias_full,
            grad_bias_out,
            depth_terms,
        ),
        ("dp", "tensor"),
    )
    return (
        layer_out,
        grad_tokens,
        grad_stack,
        grad_w_query,
        grad_w_key,
        grad_w_value,
        grad_w_output,
        grad_w_in,
        grad_w_out,
        summed[0],
        summed[1],
        summed[2],
        summed[3],
        summed[4],
        summed[5],
        summed[6],
    )


BF = jnp.bfloat16
F32 = jnp.float32
MESH = pl.DeviceIdType.MESH
BLOCK = 256
EXPONENT_SCALE = math.log2(math.e) / math.sqrt(HEAD_DIM)


PLAN = (
    (
        ("A", 0, 0, 128),
        ("A", 0, 128, 128),
        ("A", 0, 256, 128),
        ("A", 0, 384, 128),
        ("A", 0, 512, 128),
        ("B", 0, 640, 128),
        ("A", 1, 0, 128),
        ("A", 1, 128, 128),
        ("A", 1, 256, 128),
        ("B", 1, 384, 128),
        ("B", 1, 512, 128),
        ("B", 1, 640, 128),
        ("A", 2, 0, 128),
        ("A", 2, 128, 128),
        ("A", 2, 256, 128),
        ("B", 2, 384, 128),
        ("B", 2, 512, 128),
        ("B", 2, 640, 128),
    ),
    (
        ("A", 2, 0, 128),
        ("A", 2, 128, 128),
        ("A", 2, 256, 128),
        ("B", 2, 384, 128),
        ("B", 2, 512, 128),
        ("B", 2, 640, 128),
        ("A", 1, 0, 128),
        ("A", 1, 128, 128),
        ("A", 1, 256, 128),
        ("B", 1, 384, 128),
        ("B", 1, 512, 128),
        ("B", 1, 640, 128),
        ("A", 0, 0, 128),
        ("A", 0, 128, 128),
        ("A", 0, 256, 128),
        ("A", 0, 384, 128),
        ("A", 0, 512, 128),
        ("B", 0, 640, 128),
    ),
    {
        "norm": ((1, 0, 0), (1, 1, 0), (1, 2, 0), (1, 3, 0), (1, 4, 0), (1, 5, 0), (1, 6, 0), (1, 7, 0), (1, 8, 0), (1, 9, 0), (1, 10, 0), (1, 11, 0), (1, 12, 0), (1, 13, 0), (1, 15, 0), (1, 16, 0), (1, 17, 0),),
        "mask0": ((1, 5, 1), (1, 9, 1), (1, 0, 1), (1, 10, 1),),
        "mask1": ((1, 11, 1),),
        "mask2": ((1, 15, 1),),
        "mask3": ((1, 16, 1),),
        "stack0": ((1, 1, 1), (1, 17, 1),),
        "stack2": ((1, 0, 2), (1, 2, 1),),
        "proj0.0": ((1, 1, 2), (1, 3, 1), (1, 2, 2), (1, 4, 1), (1, 0, 3), (1, 3, 2), (1, 6, 1), (1, 4, 2),),
        "proj0.1": ((1, 7, 1),),
        "att0.0": ((1, 1, 3), (1, 6, 2), (1, 8, 1),),
        "att0.3": ((1, 12, 1),),
        "att1.1": ((1, 7, 2),),
        "att1.3": ((1, 2, 3), (1, 13, 1),),
        "att2.0": ((1, 8, 2),),
        "proj1.0": ((1, 12, 2), (1, 3, 3), (1, 5, 2), (1, 13, 2), (1, 4, 3),),
        "proj1.1": ((1, 9, 2), (1, 14, 0),),
        "att3.0": ((1, 5, 3),),
        "att3.3": ((1, 6, 3),),
        "att4.0": ((1, 10, 2),),
        "att5.0": ((1, 9, 3),),
        "att5.3": ((1, 7, 3), (1, 11, 2),),
        "ln2": ((1, 8, 3), (1, 10, 3), (1, 15, 2),),
        "in0": ((1, 11, 3),),
        "in2": ((1, 12, 3), (1, 16, 2),),
        "dc0": ((1, 15, 3),),
        "dc1": ((1, 13, 3), (1, 17, 2),),
        "dc2": ((0, 0, 0), (0, 1, 0), (0, 2, 0),),
        "dc3": ((1, 14, 1),),
        "bh0": ((1, 16, 3), (0, 3, 0), (0, 4, 0), (0, 5, 0), (1, 17, 3), (0, 0, 1), (1, 14, 2),),
        "bh1": ((0, 1, 1), (0, 3, 1), (0, 2, 1), (0, 4, 1), (0, 3, 2), (1, 14, 3),),
        "bh2": ((0, 3, 3), (0, 5, 1),),
        "bh3": ((0, 0, 2), (0, 4, 2),),
        "bi1": ((0, 1, 2),),
        "lnb2": ((0, 2, 2), (0, 4, 3),),
        "db0": ((0, 5, 2),),
        "db1": ((0, 0, 3),),
        "db2": ((0, 6, 0), (0, 7, 0), (0, 5, 3), (0, 8, 0),),
        "db3": ((0, 1, 3),),
        "go": ((0, 9, 0), (0, 10, 0), (0, 11, 0),),
        "dwo": ((0, 2, 3),),
        "ab0.0": ((0, 17, 0),),
        "ab0.2": ((0, 6, 1),),
        "ab1.1": ((0, 9, 1),),
        "ab1.3": ((0, 7, 1),),
        "ab2.3": ((0, 10, 1),),
        "da1": ((0, 8, 1), (0, 9, 2),),
        "ab3.0": ((0, 12, 0), (0, 13, 0), (0, 14, 0), (0, 15, 0), (0, 16, 0),),
        "ab3.2": ((0, 9, 3), (0, 11, 1),),
        "ab4.0": ((0, 10, 2),),
        "ab4.3": ((0, 17, 1),),
        "ab5.2": ((0, 6, 2), (0, 11, 2),),
        "da2": ((0, 7, 2),),
        "bp0": ((0, 12, 1), (0, 8, 2), (0, 13, 1),),
        "bp1": ((0, 17, 2),),
        "lnb1": ((0, 6, 3), (0, 14, 1), (0, 12, 2),),
        "vs0": ((0, 7, 3), (0, 13, 2),),
        "vs1": ((0, 8, 3), (0, 15, 1), (0, 14, 2),),
        "out1": ((0, 12, 3),),
        "fin": ((0, 10, 3), (0, 11, 3), (0, 13, 3), (0, 14, 3), (0, 15, 2), (0, 16, 1), (0, 17, 3),),
        "end": ((0, 15, 3), (0, 16, 2), (0, 16, 3),),
    },
)


def dot(left, right, left_axis, right_axis):
    return lax.dot_general(
        left, right, (((left_axis,), (right_axis,)), ((), ())), preferred_element_type=F32
    )


def norm_parts(values):
    centre = values - jnp.mean(values, axis=-1, keepdims=True)
    inverse = lax.rsqrt(jnp.mean(centre * centre, axis=-1, keepdims=True) + EPSILON)
    return centre * inverse, inverse


def norm_back(grad, gain, unit, inverse):
    scaled = grad * gain
    first = jnp.mean(scaled, axis=-1, keepdims=True)
    second = jnp.mean(scaled * unit, axis=-1, keepdims=True)
    return inverse * (scaled - first - unit * second)


def gelu_pair(values):
    root = math.sqrt(2.0 / math.pi)
    square = values * values
    bend = jnp.tanh(root * values * (1.0 + 0.044715 * square))
    half = 0.5 * (1.0 + bend)
    slope = half + 0.5 * root * values * (1.0 - bend * bend) * (1.0 + 3 * 0.044715 * square)
    return values * half, slope


def column_sum(values):
    return jnp.sum(values, axis=0, keepdims=True)


def rotary_tables(length):
    half = HEAD_DIM // 2
    frequency = np.exp(-np.log(10000.0) * np.arange(half) * 2.0 / HEAD_DIM)
    angles = np.arange(length)[:, None] * frequency[None, :]
    return np.cos(angles).astype(np.float32), np.sin(angles).astype(np.float32)


def fused_body(
    nz,
    rows,
    features,
    shard,
    plan,
    tokens_hbm,
    cotangent_hbm,
    stack,
    w_query,
    w_key,
    w_value,
    w_output,
    w_in,
    w_out,
    gain_one,
    shift_one,
    gain_two,
    shift_two,
    bias_in,
    bias_out,
    depth,
    starts,
    cosine_t,
    sine_t,
    layer_out,
    grad_tokens,
    grad_packed,
    grad_vectors,
    G,
    D,
    RY,
    RX,
    RZ,
    A,
    C,
    GM,
    K,
    V,
    KT,
    QT,
    OT,
    LS,
    MB,
    Z,
    GP,
    GOT,
    GT,
    WO,
    R32,
    AVG,
    SR,
    XR,
    SB,
    XG,
    VS,
    VR,
    VZ,
    GKA,
    GVA,
    tokens,
    cotangent,
    cosine,
    sine,
    BI,
    local_sem,
    ag_send,
    ag_recv,
    rs_send,
    rs_recv,
    sib_send,
    sib_recv,
    vec_send,
    vec_recv,
):
    length = 2 * rows
    heads = 3
    width = heads * HEAD_DIM
    gathers, reduces, schedule = plan
    dp = lax.axis_index("dp")
    t = lax.axis_index("tensor")
    z = dp // 2
    x = lax.rem(dp, 2)
    low = lax.rem(t, 2)
    pair = t // 2
    other = 1 - low
    sib = (dp, t + 1 - 2 * low)
    ypeer = (dp, lax.rem(t + 2, 4))
    xpeer = (dp + 1 - 2 * x, t)

    def zpeer(j):
        return (lax.rem(z + j, nz) * 2 + x, t)

    def remote(src, dst, send, recv, peer):
        return pltpu.make_async_remote_copy(
            src_ref=src, dst_ref=dst, send_sem=send, recv_sem=recv,
            device_id=peer, device_id_type=MESH,
        )

    everything = slice(None)

    def gather_copies(f, stage):
        kind, k, first, count = gathers[f]
        cols = pl.ds(first, count)
        axis = ("zxy" if kind == "A" else "yzx")[stage]
        if axis == "z":
            slot = 0 if kind == "A" else everything
            mine = G.at[k, slot, z, x, :, cols]
            sent, taken = [], []
            for j in range(nz - 1):
                sems = (ag_send.at[f, j], ag_recv.at[f, j], zpeer(j + 1))
                sent.append(lambda mine=mine, sems=sems: remote(mine, mine, *sems))
                from_z = lax.rem(z + nz - 1 - j, nz)
                taken.append(
                    lambda mine=mine, sems=sems, from_z=from_z: remote(
                        mine, G.at[k, slot, from_z, x, :, cols], *sems
                    )
                )
            return sent, taken
        if axis == "x":
            slot = 0 if kind == "A" else everything
            ref = G.at[k, slot, :, x, :, cols]
            copy = lambda: remote(ref, ref, ag_send.at[f, nz - 1], ag_recv.at[f, nz - 1], xpeer)
            return [copy], [copy]
        sems = (ag_send.at[f, nz], ag_recv.at[f, nz], ypeer)
        if kind == "A":
            copy = lambda: remote(G.at[k, 0, :, :, :, cols], G.at[k, 1, :, :, :, cols], *sems)
        else:
            copy = lambda: remote(G.at[k, 0, z, x, :, cols], G.at[k, 1, z, x, :, cols], *sems)
        return [copy], [copy]

    def gather_step(f, stage):
        if stage == 4:
            for past in range(3):
                for copy in gather_copies(f, past)[0]:
                    copy().wait_send()
            return
        if stage > 0:
            for copy in gather_copies(f, stage - 1)[1]:
                copy().wait_recv()
        if stage < 3:
            for copy in gather_copies(f, stage)[0]:
                copy().start()

    def reduce_copies(f, stage):
        kind, k, first, count = reduces[f]
        cols = pl.ds(first, count)
        axis = ("yxz" if kind == "A" else "xzy")[stage]

        def sems(n):
            return rs_send.at[f, n], rs_recv.at[f, n]

        if axis == "z":
            slot = 0 if kind == "A" else everything
            land = 0 if kind == "A" else everything
            return [
                lambda j=j: remote(
                    D.at[k, slot, lax.rem(z + j + 1, nz), x, :, cols],
                    RZ.at[k, j, land, :, cols], *sems(j), zpeer(j + 1),
                )
                for j in range(nz - 1)
            ]
        if axis == "x":
            if kind == "A":
                return [
                    lambda: remote(
                        D.at[k, 0, :, 1 - x, :, cols], RX.at[k, :, :, cols], *sems(nz - 1), xpeer
                    )
                ]
            return [
                lambda: remote(
                    D.at[k, :, :, 1 - x, :, cols], RY.at[k, :, :, :, cols], *sems(nz - 1), xpeer
                )
            ]
        if kind == "A":
            return [
                lambda side=side, n=n: remote(
                    D.at[k, 1, :, side, :, cols], RY.at[k, side, :, :, cols], *sems(nz + n), ypeer
                )
                for n, side in enumerate((1 - x, x))
            ]
        return [lambda: remote(D.at[k, 1, z, x, :, cols], RX.at[k, 0, :, cols], *sems(nz), ypeer)]

    def reduce_step(f, stage):
        kind, k, first, count = reduces[f]
        cols = pl.ds(first, count)
        if stage == 4:
            for past in range(3):
                for copy in reduce_copies(f, past):
                    copy().wait_send()
            return
        before = reduce_copies(f, stage - 1) if stage else []
        after = reduce_copies(f, stage) if stage < 3 else []

        def add(target, source):
            target[...] = (target[...].astype(F32) + source[...].astype(F32)).astype(BF)

        if kind == "A" and stage == 1:
            before[0]().wait_recv()
            add(D.at[k, 0, :, 1 - x, :, cols], RY.at[k, 1 - x, :, :, cols])
            after[0]().start()
            before[1]().wait_recv()
            add(D.at[k, 0, :, x, :, cols], RY.at[k, x, :, :, cols])
            return
        for copy in before:
            copy().wait_recv()
        if kind == "A" and stage == 2:
            add(D.at[k, 0, :, x, :, cols], RX.at[k, :, :, cols])
        elif kind == "B" and stage == 1:
            add(D.at[k, :, :, x, :, cols], RY.at[k, :, :, :, cols])
        elif kind == "B" and stage == 2:
            total = D[k, :, z, x, :, cols].astype(F32)
            for j in range(nz - 1):
                total = total + RZ[k, j, :, :, cols].astype(F32)
            D[k, 1, z, x, :, cols] = total[1].astype(BF)
            grad_packed[k, :, cols] = total[0]
        elif kind == "A" and stage == 3:
            total = D[k, 0, z, x, :, cols].astype(F32)
            for j in range(nz - 1):
                total = total + RZ[k, j, 0, :, cols].astype(F32)
            grad_packed[k, :, cols] = total
        elif kind == "B" and stage == 3:
            grad_packed[k, :, cols] = grad_packed[k, :, cols] + RX[k, 0, :, cols].astype(F32)
        for copy in after:
            copy().start()

    def tick(name):
        for gather, flow, stage in schedule.get(name, ()):
            if gather:
                gather_step(flow, stage)
            else:
                reduce_step(flow, stage)

    def tick_at(prefix, index, count, suffix=""):
        for i in range(count):
            name = prefix + str(i) + suffix
            if schedule.get(name):

                @pl.when(index == i)
                def _(name=name):
                    tick(name)

    def sib_copy(n, src, dst):
        return remote(src, dst, sib_send.at[n], sib_recv.at[n], sib)

    send_a = sib_copy(0, A.at[low], A.at[low])
    take_a = sib_copy(0, A.at[low], A.at[other])
    send_gm = sib_copy(1, GM.at[low], GM.at[low])
    take_gm = sib_copy(1, GM.at[low], GM.at[other])
    part_r = sib_copy(2, SR, XR)
    send_c = sib_copy(3, C.at[low], C.at[low])
    take_c = sib_copy(3, C.at[low], C.at[other])
    part_g = sib_copy(4, SB, XG)
    send_gl = sib_copy(5, GM.at[low], GM.at[low])
    take_gl = sib_copy(5, GM.at[low], GM.at[other])
    part_b = sib_copy(6, SB, XG)
    part_a = sib_copy(7, SB, XG)

    loads = [
        pltpu.make_async_copy(tokens_hbm, tokens, local_sem.at[0]),
        pltpu.make_async_copy(cotangent_hbm, cotangent, local_sem.at[1]),
        pltpu.make_async_copy(stack, Z, local_sem.at[2]),
    ]
    for load in loads:
        load.start()
    barrier = pltpu.get_barrier_semaphore()
    partners = [sib, ypeer, xpeer] + [zpeer(j + 1) for j in range(nz - 1)]
    for peer in partners:
        pl.semaphore_signal(barrier, inc=1, device_id=peer, device_id_type=MESH)
    G[0, 0, z, x] = jnp.concatenate(
        [w_query[...], w_key[...], w_value[...], w_output[...].T], axis=1
    )
    G[1, 0, z, x] = w_in[...]
    G[2, 0, z, x] = w_out[...].T
    pl.semaphore_wait(barrier, len(partners))
    tick("norm")

    gain_one, shift_one = gain_one[...], shift_one[...]
    gain_two, shift_two = gain_two[...], shift_two[...]
    piece = 128
    pieces = rows // piece

    def chunk(i):
        return pl.ds(pl.multiple_of(i * piece, piece), piece)

    loads[0].wait()
    loads[1].wait()

    def first_norm(i, carry):
        unit, _ = norm_parts(tokens[chunk(i), :].astype(F32))
        A[low, chunk(i), :] = (unit * gain_one + shift_one).astype(BF)
        GM[low, chunk(i), :] = (depth[4] * cotangent[chunk(i), :].astype(F32)).astype(BF)
        return carry

    lax.fori_loop(0, pieces, first_norm, 0)
    send_a.start()
    send_gm.start()
    for n in range(4):
        BI[n : n + 1, :] = bias_in[:, n * features : (n + 1) * features]
    cosine[...] = jnp.concatenate([cosine_t[...]] * 4, axis=0).T
    sine[...] = jnp.concatenate([-sine_t[...], sine_t[...]] * 2, axis=0).T

    s0, s1 = starts[pair, 0], starts[pair, 1]
    blocks = length // BLOCK
    for block in range(blocks):
        tick("mask" + str(block))
        key = block * BLOCK + lax.broadcasted_iota(jnp.int32, (2 * BLOCK, BLOCK), 0)
        query = block * BLOCK + lax.broadcasted_iota(jnp.int32, (2 * BLOCK, BLOCK), 1)
        fine = key <= query
        for s in (s0, s1):
            fine = fine | ((key >= s) & (key < s + PIECE) & (query >= s) & (query < s + PIECE))
        MB[block] = jnp.where(fine, 0.0, NEGATIVE)
    VS[...] = jnp.zeros_like(VS)
    for s in range(2):
        for h in range(heads):
            V[heads * s + h, :, HEAD_DIM:] = jnp.where(
                lax.broadcasted_iota(jnp.int32, (length, HEAD_DIM), 1) == 0, 1.0, 0.0
            ).astype(BF)

    loads[2].wait()

    def earlier(i, sums):
        tick_at("stack", i, pieces)
        grad = cotangent[chunk(i), :].astype(F32)
        mean = jnp.zeros((piece, features), F32)
        new = [sums[0] + column_sum(grad)]
        for k in range(4):
            layer = Z[k, chunk(i), :].astype(F32)
            mean = mean + depth[k] * layer
            new.append(sums[k + 1] + column_sum(layer * grad))
        AVG[chunk(i), :] = mean
        return tuple(new)

    zero_row = jnp.zeros((1, features), F32)
    sums = lax.fori_loop(0, pieces, earlier, (zero_row,) * 5)
    VS[4:5, :] = depth[4] * sums[0]
    for k in range(4):
        VS[5 + k : 6 + k, :] = sums[k + 1]

    take_a.wait_recv()

    def whole(ref, *index):
        value = ref[index]
        return value.reshape(value.shape[-4] * value.shape[-3] * value.shape[-2], value.shape[-1])

    lane = lax.broadcasted_iota(jnp.int32, (rows, 128), 1)
    front = lax.rem(lane, HEAD_DIM) < HEAD_DIM // 2

    def project(slot):
        for half in range(2):
            tick_at("proj", slot, 2, "." + str(half))
            weight = whole(G, 0, slot, everything, everything, everything, slice(0, 640))
            span = slice(half * rows, (half + 1) * rows)
            result = dot(A[half], weight, 1, 0)
            turned = []
            for tile in range(3):
                part = result[:, tile * 128 : (tile + 1) * 128]
                partner = jnp.where(front, pltpu.roll(part, 96, 1), pltpu.roll(part, 32, 1))
                turned.append((part * cosine[span, :] + partner * sine[span, :]).astype(BF))
            for h in range(heads):
                n = heads * slot + h
                at = h * HEAD_DIM
                QT[n, :, span] = turned[at // 128][:, at % 128 : at % 128 + HEAD_DIM].T
                at = width + h * HEAD_DIM
                key = turned[at // 128][:, at % 128 : at % 128 + HEAD_DIM]
                K[n, span, :] = key
                KT[n, :, span] = key.T
                at = 2 * width + h * HEAD_DIM
                V[n, span, :HEAD_DIM] = result[:, at : at + HEAD_DIM].astype(BF)

    def attend(n, carry):
        @pl.when(lax.rem(n, heads) == 0)
        def _():
            project(n // heads)

        for block in range(blocks):
            tick_at("att", n, 2 * heads, "." + str(block))
            lo = block * BLOCK
            top = min(lo + 2 * BLOCK, length)
            half, at = lo // rows, lo % rows
            score = dot(K[n, 0:top, :], QT[n, :, lo : lo + BLOCK], 1, 0) * EXPONENT_SCALE
            tail = score[lo:] + MB[block, 0 : top - lo, :]
            score = jnp.concatenate([score[:lo], tail], axis=0) if lo else tail
            highest = jnp.max(score, axis=0, keepdims=True)
            power = jnp.exp2(score - highest).astype(BF)
            mixed = dot(V[n, 0:top, :], power, 0, 0)
            total = mixed[HEAD_DIM : HEAD_DIM + 1, :]
            OT[half, n, :, at : at + BLOCK] = (mixed[:HEAD_DIM, :] / total).astype(BF)
            LS[n, :, lo : lo + BLOCK] = highest + jnp.log2(total)
        return carry

    lax.fori_loop(0, 2 * heads, attend, 0)
    tick("wo")
    for slot in range(2):
        flipped = whole(G, 0, slot, everything, everything, everything, slice(512, 768)).T
        WO[slot * width : (slot + 1) * width, :] = flipped[64:256, :]

    def mixed_rows(half):
        return OT[half].reshape(2 * width, rows)

    tick("r.other")
    SR[...] = dot(mixed_rows(other), WO[...], 0, 0)
    part_r.start()
    tick("r.low")
    R32[...] = dot(mixed_rows(low), WO[...], 0, 0)
    part_r.wait_recv()
    tick("ln2")

    def second_norm(i, carry):
        middle = tokens[chunk(i), :].astype(F32) + R32[chunk(i), :] + XR[chunk(i), :]
        R32[chunk(i), :] = middle
        unit, _ = norm_parts(middle)
        C[low, chunk(i), :] = (unit * gain_two + shift_two).astype(BF)
        return carry

    lax.fori_loop(0, pieces, second_norm, 0)
    send_c.start()
    def hidden_bias(slot):
        return BI[pl.ds(lax.rem(t + 2 * slot, 4), 1), :]

    def inner(i, carry):
        tick_at("in", i, 4)

        @pl.when(i == 2)
        def _():
            take_c.wait_recv()

        half, slot = lax.rem(low + i // 2, 2), lax.rem(i, 2)
        pre = dot(C[half], whole(G, 1, slot), 1, 0) + hidden_bias(slot)
        act, slope = gelu_pair(pre)
        Z[2 * slot + half] = act.astype(BF)
        GP[2 * slot + half] = slope.astype(BF)
        return carry

    lax.fori_loop(0, 4, inner, 0)
    take_gm.wait_recv()

    def outer_products(name, k, left, right):
        half_rows = features // 2

        def one(i, carry):
            tick_at(name, i, 4)
            slot, part = 1 - i // 2, lax.rem(i, 2)
            cols = pl.ds(pl.multiple_of(part * half_rows, 128), half_rows)
            value = dot(
                left[:, :, cols].reshape(length, half_rows),
                right[pl.ds(2 * slot, 2)].reshape(length, features),
                0,
                0,
            )
            D[k, slot, pl.ds(part * (nz // 2), nz // 2)] = value.astype(BF).reshape(
                nz // 2, 2, shard, features
            )
            return carry

        lax.fori_loop(0, 4, one, 0)

    outer_products("dc", 2, GM, Z)

    def back(i, carry):
        half = lax.rem(other + i, 2)

        def one(slot, total):
            tick_at("bh", 2 * i + slot, 4)
            grad = dot(GM[half], whole(G, 2, slot), 1, 0)
            total = total + column_sum(grad * Z[2 * slot + half].astype(F32))
            grad = (grad * GP[2 * slot + half].astype(F32)).astype(BF)
            GP[2 * slot + half] = grad
            row = pl.ds(9 + lax.rem(t + 2 * slot, 4), 1)
            VS[row, :] = VS[row, :] + column_sum(grad.astype(F32))
            return total

        carry = lax.fori_loop(0, 2, one, carry)
        tick_at("bi", i, 2)
        grad_tokens[...] = dot(GP[half], whole(G, 1, 0), 1, 1) + dot(
            GP[2 + half], whole(G, 1, 1), 1, 1
        )

        @pl.when(i == 0)
        def _():
            SB[...] = grad_tokens[...].astype(BF)
            part_g.start()

        return carry

    VS[13:14, :] = lax.fori_loop(0, 2, back, zero_row) / depth[4]
    part_g.wait_recv()
    send_gm.wait_send()
    tick("lnb2")

    def second_back(i, carry):
        middle = R32[chunk(i), :]
        unit, inverse = norm_parts(middle)
        grad = grad_tokens[chunk(i), :] + XG[chunk(i), :].astype(F32)
        coming = cotangent[chunk(i), :].astype(F32)
        whole_grad = depth[4] * coming + norm_back(grad, gain_two, unit, inverse)
        grad_tokens[chunk(i), :] = whole_grad
        GM[low, chunk(i), :] = whole_grad.astype(BF)
        return (
            carry[0] + column_sum(grad * unit),
            carry[1] + column_sum(grad),
            carry[2] + column_sum(coming * (middle + bias_out[...])),
        )

    sums = lax.fori_loop(0, pieces, second_back, (zero_row,) * 3)
    VS[2:3, :] = sums[0]
    VS[3:4, :] = sums[1]
    send_gl.start()
    VS[13:14, :] = VS[13:14, :] + sums[2]
    outer_products("db", 1, C, GP)

    take_gl.wait_recv()
    tick("go")

    def grad_mixed(half, carry):
        GOT[half] = dot(WO[...], GM[half], 1, 1).astype(BF).reshape(2 * heads, HEAD_DIM, rows)
        return carry

    lax.fori_loop(0, 2, grad_mixed, 0)
    tick("dwo")
    for slot in range(2):
        value = sum(
            dot(OT[half, heads * slot : heads * slot + heads].reshape(width, rows), GM[half], 1, 0)
            for half in range(2)
        )
        D[0, slot, :, :, :, 3 * width :] = value.T.astype(BF).reshape(nz, 2, shard, width)

    def unturn(value, span):
        front_half, back_half = value[: HEAD_DIM // 2], value[HEAD_DIM // 2 :]
        cosines, sines = cosine_t[:, span], sine_t[:, span]
        return jnp.concatenate(
            [front_half * cosines + back_half * sines, back_half * cosines - front_half * sines],
            axis=0,
        )

    scale = 1.0 / math.sqrt(HEAD_DIM)

    def attend_back(i, carry):
        slot, h = 1 - i // heads, lax.rem(i, heads)
        n = heads * slot + h

        def place(which):
            return pl.ds(pl.multiple_of(which * width + h * HEAD_DIM, HEAD_DIM), HEAD_DIM)

        GKA[...] = jnp.zeros_like(GKA)
        GVA[...] = jnp.zeros_like(GVA)
        for block in range(blocks):
            tick_at("ab", i, 2 * heads, "." + str(block))
            lo = block * BLOCK
            top = min(lo + 2 * BLOCK, length)
            half, at = lo // rows, lo % rows
            here = slice(at, at + BLOCK)
            grad_t = GOT[half, n, :, here]
            delta = jnp.sum(
                OT[half, n, :, here].astype(F32) * grad_t.astype(F32), axis=0, keepdims=True
            )
            score = dot(K[n, 0:top, :], QT[n, :, lo : lo + BLOCK], 1, 0) * EXPONENT_SCALE
            score = score - LS[n, :, lo : lo + BLOCK]
            tail = score[lo:] + MB[block, 0 : top - lo, :]
            score = jnp.concatenate([score[:lo], tail], axis=0) if lo else tail
            power = jnp.exp2(score)
            grad_power = dot(V[n, 0:top, :HEAD_DIM], grad_t, 1, 0)
            grad_score = (power * (grad_power - delta)).astype(BF)
            GVA[:, 0:top] += dot(grad_t, power.astype(BF), 1, 1)
            GKA[:, 0:top] += dot(QT[n, :, lo : lo + BLOCK], grad_score, 1, 1)
            grad_query = dot(KT[n, :, 0:top], grad_score, 1, 0) * scale
            GT[slot, half, place(0), here] = unturn(grad_query, slice(lo, lo + BLOCK)).astype(BF)
        for half in range(2):
            span = slice(half * rows, (half + 1) * rows)
            GT[slot, half, place(1), :] = unturn(GKA[:, span] * scale, span).astype(BF)
            GT[slot, half, place(2), :] = GVA[:, span].astype(BF)

        @pl.when(h == heads - 1)
        def _():
            for part in range(2):
                tick_at("da", 2 * (1 - slot) + part, 4)
                half_rows = features // 2
                cols = slice(part * half_rows, (part + 1) * half_rows)
                value = dot(A[0, :, cols], GT[slot, 0], 0, 1) + dot(
                    A[1, :, cols], GT[slot, 1], 0, 1
                )
                first = part * (nz // 2)
                D[0, slot, first : first + nz // 2, :, :, : 3 * width] = value.astype(BF).reshape(
                    nz // 2, 2, shard, 3 * width
                )

        return carry

    lax.fori_loop(0, 2 * heads, attend_back, 0)

    def back_project(half):
        return sum(dot(GT[s, half], whole(G, 0, s)[:, : 3 * width], 0, 1) for s in range(2))

    part_g.wait_send()
    part_r.wait_send()

    def back_projects(i, carry):
        tick_at("bp", i, 2)
        SR[...] = back_project(lax.rem(other + i, 2))

        @pl.when(i == 0)
        def _():
            SB[...] = SR[...].astype(BF)
            part_a.start()

        return carry

    lax.fori_loop(0, 2, back_projects, 0)
    part_a.wait_recv()
    tick("lnb1")

    def first_back(i, carry):
        unit, inverse = norm_parts(tokens[chunk(i), :].astype(F32))
        grad = SR[chunk(i), :] + XG[chunk(i), :].astype(F32)
        grad_tokens[chunk(i), :] = grad_tokens[chunk(i), :] + norm_back(grad, gain_one, unit, inverse)
        return (carry[0] + column_sum(grad * unit), carry[1] + column_sum(grad))

    sums = lax.fori_loop(0, pieces, first_back, (zero_row, zero_row))
    VS[0:1, :] = sums[0]
    VS[1:2, :] = sums[1]

    def vector_round(n, src, peer):
        copy = remote(src, VR.at[n], vec_send.at[n], vec_recv.at[n], peer)
        copy.start()
        return copy

    round_s = vector_round(0, VS, sib)
    tick("vs0")
    round_s.wait_recv()
    VZ[nz] = VS[...] + VR[0]
    round_y = vector_round(1, VZ.at[nz], ypeer)
    tick("vs1")

    part_a.wait_send()

    def outer(half):
        return dot(Z[half], whole(G, 2, 0), 1, 1) + dot(Z[2 + half], whole(G, 2, 1), 1, 1)

    def outers(i, carry):
        tick_at("out", i, 2)
        SR[...] = outer(lax.rem(other + i, 2))

        @pl.when(i == 0)
        def _():
            SB[...] = SR[...].astype(BF)
            part_b.start()

        return carry

    lax.fori_loop(0, 1, outers, 0)
    round_y.wait_recv()
    VZ[nz + 1] = VZ[nz] + VR[1]
    round_x = vector_round(2, VZ.at[nz + 1], xpeer)
    lax.fori_loop(1, 2, outers, 0)
    part_b.wait_recv()
    round_x.wait_recv()
    VZ[z] = VZ[nz + 1] + VR[2]
    rounds_z = [
        remote(VZ.at[z], VZ.at[z], vec_send.at[3 + j], vec_recv.at[3 + j], zpeer(j + 1))
        for j in range(nz - 1)
    ]
    for c in rounds_z:
        c.start()
    tick("fin")

    def finish_block(i, carry):
        value = R32[chunk(i), :] + SR[chunk(i), :] + XG[chunk(i), :].astype(F32) + bias_out[...]
        layer_out[chunk(i), :] = (AVG[chunk(i), :] + depth[4] * value).astype(BF)
        return carry

    lax.fori_loop(0, pieces, finish_block, 0)
    tick("vs2")
    for j in range(nz - 1):
        remote(
            VZ.at[z], VZ.at[lax.rem(z + nz - 1 - j, nz)],
            vec_send.at[3 + j], vec_recv.at[3 + j], zpeer(j + 1),
        ).wait_recv()
    total = VZ[0]
    for j in range(1, nz):
        total = total + VZ[j]
    grad_vectors[...] = total
    for f in range(len(gathers)):
        gather_step(f, 4)
    tick("end")
    for f in range(len(reduces)):
        reduce_step(f, 4)
    for c in [send_a, send_c, send_gl, part_b, round_s, round_y, round_x] + rounds_z:
        c.wait_send()


def spread_body(width, cotangent, packed, sums, depth, stack, wq, wk, wv, wo, wi, wu, *rest):
    for k in range(4):
        stack[k] = depth[k] * cotangent[...].astype(F32)

    @pl.when(pl.program_id(0) == 0)
    def _():
        gain_one, shift_one, gain_two, shift_two, bias_in, bias_out, grad_depth = rest
        for n, ref in enumerate((wq, wk, wv)):
            ref[...] = packed[0, :, n * width : (n + 1) * width]
        wo[...] = packed[0, :, 3 * width :].T
        wi[...] = packed[1]
        wu[...] = packed[2].T
        for n, ref in enumerate((gain_one, shift_one, gain_two, shift_two, bias_out)):
            ref[...] = sums[n : n + 1, :]
        bias_in[...] = jnp.concatenate([sums[9 + n : 10 + n, :] for n in range(4)], axis=1)
        lane = lax.broadcasted_iota(jnp.int32, (1, 5), 1)
        total = jnp.zeros((1, 5), F32)
        for n, row in enumerate((5, 6, 7, 8, 13)):
            total = jnp.where(lane == n, jnp.sum(sums[row : row + 1, :]), total)
        grad_depth[...] = total


def fused_device(
    tokens,
    stack,
    cotangent,
    starts,
    w_query,
    w_key,
    w_value,
    w_output,
    w_in,
    w_out,
    gain_one,
    shift_one,
    gain_two,
    shift_two,
    bias_in,
    bias_out,
    depth_weights,
):
    rows, features = tokens.shape
    shard = w_query.shape[0]
    nz = lax.axis_size("dp") // 2
    length = 2 * rows
    width = w_query.shape[1]
    heads = width // HEAD_DIM
    cos_np, sin_np = rotary_tables(length)
    gathers, reduces, schedule = PLAN
    shape = jax.ShapeDtypeStruct
    vmem = pl.BlockSpec(memory_space=pltpu.VMEM)
    smem = pl.BlockSpec(memory_space=pltpu.SMEM)
    hbm = pl.BlockSpec(memory_space=pl.ANY)
    dma = pltpu.SemaphoreType.DMA
    scratch = [
        pltpu.VMEM((3, 2, nz, 2, shard, features), BF),
        pltpu.VMEM((3, 2, nz, 2, shard, features), BF),
        pltpu.VMEM((3, 2, nz, shard, features), BF),
        pltpu.VMEM((3, nz, shard, features), BF),
        pltpu.VMEM((3, nz - 1, 2, shard, features), BF),
        pltpu.VMEM((2, rows, features), BF),
        pltpu.VMEM((2, rows, features), BF),
        pltpu.VMEM((2, rows, features), BF),
        pltpu.VMEM((2 * heads, length, HEAD_DIM), BF),
        pltpu.VMEM((2 * heads, length, 2 * HEAD_DIM), BF),
        pltpu.VMEM((2 * heads, HEAD_DIM, length), BF),
        pltpu.VMEM((2 * heads, HEAD_DIM, length), BF),
        pltpu.VMEM((2, 2 * heads, HEAD_DIM, rows), BF),
        pltpu.VMEM((2 * heads, 1, length), F32),
        pltpu.VMEM((length // BLOCK, 2 * BLOCK, BLOCK), F32),
        pltpu.VMEM((4, rows, features), BF),
        pltpu.VMEM((4, rows, features), BF),
        pltpu.VMEM((2, 2 * heads, HEAD_DIM, rows), BF),
        pltpu.VMEM((2, 2, 3 * width, rows), BF),
        pltpu.VMEM((2 * width, features), BF),
        pltpu.VMEM((rows, features), F32),
        pltpu.VMEM((rows, features), F32),
        pltpu.VMEM((rows, features), F32),
        pltpu.VMEM((rows, features), F32),
        pltpu.VMEM((rows, features), BF),
        pltpu.VMEM((rows, features), BF),
        pltpu.VMEM((16, features), F32),
        pltpu.VMEM((3, 16, features), F32),
        pltpu.VMEM((nz + 2, 16, features), F32),
        pltpu.VMEM((HEAD_DIM, length), F32),
        pltpu.VMEM((HEAD_DIM, length), F32),
        pltpu.VMEM((rows, features), BF),
        pltpu.VMEM((rows, features), BF),
        pltpu.VMEM((length, 2 * HEAD_DIM), F32),
        pltpu.VMEM((length, 2 * HEAD_DIM), F32),
        pltpu.VMEM((4, features), F32),
        dma((3,)),
        dma((len(gathers), nz + 1)),
        dma((len(gathers), nz + 1)),
        dma((len(reduces), nz + 2)),
        dma((len(reduces), nz + 2)),
        dma((8,)),
        dma((8,)),
        dma((nz + 2,)),
        dma((nz + 2,)),
    ]

    def row(vector):
        return vector.reshape(1, -1)

    layer_out, grad_tokens, packed, sums = pl.pallas_call(
        functools.partial(fused_body, nz, rows, features, shard, PLAN),
        out_shape=[
            shape((rows, features), BF),
            shape((rows, features), F32),
            shape((3, shard, features), F32),
            shape((16, features), F32),
        ],
        in_specs=[hbm] * 3 + [vmem] * 12 + [smem] * 2 + [vmem] * 2,
        out_specs=[vmem] * 4,
        scratch_shapes=scratch,
        compiler_params=pltpu.CompilerParams(
            collective_id=0, has_side_effects=True, vmem_limit_bytes=64 * 1024 * 1024
        ),
    )(
        tokens,
        cotangent,
        stack,
        w_query,
        w_key,
        w_value,
        w_output,
        w_in,
        w_out,
        row(gain_one),
        row(shift_one),
        row(gain_two),
        row(shift_two),
        row(bias_in),
        row(bias_out),
        depth_weights,
        starts,
        jnp.asarray(cos_np.T.copy()),
        jnp.asarray(sin_np.T.copy()),
    )

    part = rows // 4
    sizes = (
        [(shard, width)] * 3
        + [(width, shard), (shard, features), (features, shard)]
        + [(1, features)] * 4
        + [(1, 4 * features), (1, features), (1, 5)]
    )

    def fixed(size):
        return pl.BlockSpec(size, lambda i: (0,) * len(size))

    outs = pl.pallas_call(
        functools.partial(spread_body, width),
        grid=(4,),
        out_shape=[shape((4, rows, features), F32)] + [shape(size, F32) for size in sizes],
        in_specs=[
            pl.BlockSpec((part, features), lambda i: (i, 0)),
            fixed((3, shard, features)),
            fixed((16, features)),
            smem,
        ],
        out_specs=[pl.BlockSpec((4, part, features), lambda i: (0, i, 0))]
        + [fixed(size) for size in sizes],
        compiler_params=pltpu.CompilerParams(vmem_limit_bytes=32 * 1024 * 1024),
    )(cotangent, packed, sums, depth_weights)
    return (layer_out, grad_tokens, *outs[:7], *[vector.reshape(-1) for vector in outs[7:]])


def per_device(*arrays):
    rows, features = arrays[0].shape
    shard, width = arrays[4].shape
    dp = lax.axis_size("dp")
    fits = (
        shard % 16 == 0
        and dp % 4 == 0
        and lax.axis_size("tensor") == 4
        and arrays[3].shape[0] == 2
        and arrays[8].shape[1] == features
        and 4 * width == features
        and shard * dp == features
    )
    return fused_device(*arrays) if fits else plain_device(*arrays)


def solution(mesh):
    in_specs = (
        P(("dp", "tensor"), None),
        P(None, ("dp", "tensor"), None),
        P(("dp", "tensor"), None),
        P("dp", None),
        P("dp", "tensor"),
        P("dp", "tensor"),
        P("dp", "tensor"),
        P("tensor", "dp"),
        P("dp", "tensor"),
        P("tensor", "dp"),
        P(),
        P(),
        P(),
        P(),
        P(),
        P(),
        P(),
    )
    out_specs = (
        P(("dp", "tensor"), None),
        P(("dp", "tensor"), None),
        P(None, ("dp", "tensor"), None),
        P("dp", "tensor"),
        P("dp", "tensor"),
        P("dp", "tensor"),
        P("tensor", "dp"),
        P("dp", "tensor"),
        P("tensor", "dp"),
        P(),
        P(),
        P(),
        P(),
        P(),
        P(),
        P(),
    )
    return jax.shard_map(
        per_device, mesh=mesh, in_specs=in_specs, out_specs=out_specs, check_vma=False
    )
```

profile of v0, /device:TPU:0, one launch (start us, length us, event | category | flops | bytes accessed | tf_op | source)
XLA Modules:
  0.0 190.2 jit_solution(17395123477137210056)
XLA Ops:
  0.6 1.3 reshape.71.gain_one
  1.9 1.3 reshape.72.shift_one
  3.2 1.3 reshape.73.gain_two
  4.4 1.3 reshape.74.shift_two
  5.7 1.3 reshape.76.bias_out
  7.0 1.7 copy.35.w_out
  8.7 166.5 %shard_map.306 = (bf16[512,768]{1,0:T(8,128)(2,1)}, f32[512,768]{1,0:T(8,128)}, f32[3,96,768]{2,1,0:T(8,128)}, f32[16,768]{1,0:T(8,128)}) custom-call(bf16[512,768]{1,0:T(8,128)(2,1)} %tokens_hbm.1, bf16[512,768]{1,0:T(8,128)(2,1)} %cotangent.1, bf16[4,512,768]{2,1,0:T(8,128)(2,1)} %stack.1, bf16[96,192]{1,0:T(8,128)(2,1)} %w_query.1, ...), custom_call_target="tpu_custom_call" | custom-call | tf_op jit(solution)/shard_map/pallas_call | solution.py:1248
  175.2 0.0 copy-start
  175.2 1.1 copy-done
  176.4 0.0 copy-start.1
  176.4 1.2 copy-done.1
  177.5 0.0 copy-start.2
  177.5 0.8 copy-done.2
  178.3 0.7 copy-done.3
  179.0 4.1 %shard_map.307 = (f32[4,512,768]{2,1,0:T(8,128)}, f32[96,192]{1,0:T(8,128)}, f32[96,192]{1,0:T(8,128)}, f32[96,192]{1,0:T(8,128)}, f32[192,96]{1,0:T(8,128)}, /*...) custom-call(bf16[512,768]{1,0:T(8,128)(2,1)S(1)} %copy-done, ...), custom_call_target="tpu_custom_call" | custom-call | tf_op jit(solution)/shard_map/pallas_call | solution.py:1295
  183.1 0.6 reduce
  183.7 0.6 reduce.1
  184.3 0.6 reduce.2
  184.9 0.6 reduce.3
  185.5 0.6 reduce.4
  186.1 0.9 copy.36
  187.0 2.1 %copy.39 = bf16[512,768]{1,0:T(8,128)(2,1)} copy(bf16[512,768]{1,0:T(8,128)(2,1)} %get-tuple-element.84) | data formatting | bytes 1572864
  189.0 0.0 copy-done.4
  189.0 1.1 copy.40
  (2 shorter events, 0.0 us)
Async XLA Ops:
  175.2 1.1 copy-start
  176.4 1.2 copy-start.1
  177.5 0.8 copy-start.2
  178.3 0.7 copy-start.3
  179.0 10.0 %copy-start.4 = (f32[512,768]{1,0:T(8,128)S(1)}, f32[512,768]{1,0:T(8,128)}, u32[]{:S(2)}) copy-start(f32[512,768]{1,0:T(8,128)} %get-tuple-element.85) | copy-start | bytes 4718596
where the time goes:
time: 191 us; the launch traced here: 190 us
  Pallas kernels  171 us (90%)
  local copies, waits for them, and re-layouts  15.9 us (8%)
  other arithmetic  3.03 us (2%)
    pallas_call x1, Pallas kernels, fused_device(): pl.pallas_call(functools.partial(fused_body, nz, rows, features, shard, P...  167 us
    unnamed x14, local copies, waits for them, and re-layouts  9.55 us
    reshape x5, local copies, waits for them, and re-layouts, row(): return vector.reshape(1, -1)  6.33 us
    pallas_call x1, Pallas kernels, fused_device(): pl.pallas_call(functools.partial(spread_body, width), grid=(4,), out_shap...  4.05 us

commit v1 on v0

--- a/solution.py
+++ b/solution.py
@@ -313,100 +313,99 @@
         ("A", 0, 384, 128),
         ("A", 0, 512, 128),
         ("B", 0, 640, 128),
-        ("A", 1, 0, 128),
-        ("A", 1, 128, 128),
-        ("A", 1, 256, 128),
-        ("B", 1, 384, 128),
-        ("B", 1, 512, 128),
+        ("A", 1, 0, 256),
+        ("B", 1, 256, 128),
+        ("A", 1, 384, 128),
+        ("A", 1, 512, 128),
         ("B", 1, 640, 128),
         ("A", 2, 0, 128),
-        ("A", 2, 128, 128),
+        ("B", 2, 128, 128),
         ("A", 2, 256, 128),
-        ("B", 2, 384, 128),
+        ("A", 2, 384, 128),
         ("B", 2, 512, 128),
         ("B", 2, 640, 128),
     ),
     (
-        ("A", 2, 0, 128),
-        ("A", 2, 128, 128),
-        ("A", 2, 256, 128),
-        ("B", 2, 384, 128),
-        ("B", 2, 512, 128),
+        ("B", 2, 0, 128),
+        ("B", 2, 128, 128),
+        ("A", 2, 256, 256),
+        ("A", 2, 512, 128),
         ("B", 2, 640, 128),
-        ("A", 1, 0, 128),
-        ("A", 1, 128, 128),
-        ("A", 1, 256, 128),
-        ("B", 1, 384, 128),
-        ("B", 1, 512, 128),
-        ("B", 1, 640, 128),
-        ("A", 0, 0, 128),
-        ("A", 0, 128, 128),
+        ("B", 1, 0, 128),
+        ("B", 1, 128, 128),
+        ("B", 1, 256, 128),
+        ("A", 1, 384, 128),
+        ("A", 1, 512, 128),
+        ("A", 1, 640, 128),
+        ("A", 0, 0, 256),
         ("A", 0, 256, 128),
         ("A", 0, 384, 128),
         ("A", 0, 512, 128),
         ("B", 0, 640, 128),
     ),
     {
-        "norm": ((1, 0, 0), (1, 1, 0), (1, 2, 0), (1, 3, 0), (1, 4, 0), (1, 5, 0), (1, 6, 0), (1, 7, 0), (1, 8, 0), (1, 9, 0), (1, 10, 0), (1, 11, 0), (1, 12, 0), (1, 13, 0), (1, 15, 0), (1, 16, 0), (1, 17, 0),),
-        "mask0": ((1, 5, 1), (1, 9, 1), (1, 0, 1), (1, 10, 1),),
-        "mask1": ((1, 11, 1),),
-        "mask2": ((1, 15, 1),),
-        "mask3": ((1, 16, 1),),
-        "stack0": ((1, 1, 1), (1, 17, 1),),
-        "stack2": ((1, 0, 2), (1, 2, 1),),
-        "proj0.0": ((1, 1, 2), (1, 3, 1), (1, 2, 2), (1, 4, 1), (1, 0, 3), (1, 3, 2), (1, 6, 1), (1, 4, 2),),
-        "proj0.1": ((1, 7, 1),),
-        "att0.0": ((1, 1, 3), (1, 6, 2), (1, 8, 1),),
-        "att0.3": ((1, 12, 1),),
-        "att1.1": ((1, 7, 2),),
-        "att1.3": ((1, 2, 3), (1, 13, 1),),
-        "att2.0": ((1, 8, 2),),
-        "proj1.0": ((1, 12, 2), (1, 3, 3), (1, 5, 2), (1, 13, 2), (1, 4, 3),),
-        "proj1.1": ((1, 9, 2), (1, 14, 0),),
-        "att3.0": ((1, 5, 3),),
-        "att3.3": ((1, 6, 3),),
-        "att4.0": ((1, 10, 2),),
-        "att5.0": ((1, 9, 3),),
-        "att5.3": ((1, 7, 3), (1, 11, 2),),
-        "ln2": ((1, 8, 3), (1, 10, 3), (1, 15, 2),),
-        "in0": ((1, 11, 3),),
-        "in2": ((1, 12, 3), (1, 16, 2),),
-        "dc0": ((1, 15, 3),),
-        "dc1": ((1, 13, 3), (1, 17, 2),),
-        "dc2": ((0, 0, 0), (0, 1, 0), (0, 2, 0),),
-        "dc3": ((1, 14, 1),),
-        "bh0": ((1, 16, 3), (0, 3, 0), (0, 4, 0), (0, 5, 0), (1, 17, 3), (0, 0, 1), (1, 14, 2),),
-        "bh1": ((0, 1, 1), (0, 3, 1), (0, 2, 1), (0, 4, 1), (0, 3, 2), (1, 14, 3),),
-        "bh2": ((0, 3, 3), (0, 5, 1),),
-        "bh3": ((0, 0, 2), (0, 4, 2),),
-        "bi1": ((0, 1, 2),),
-        "lnb2": ((0, 2, 2), (0, 4, 3),),
-        "db0": ((0, 5, 2),),
-        "db1": ((0, 0, 3),),
-        "db2": ((0, 6, 0), (0, 7, 0), (0, 5, 3), (0, 8, 0),),
-        "db3": ((0, 1, 3),),
-        "go": ((0, 9, 0), (0, 10, 0), (0, 11, 0),),
-        "dwo": ((0, 2, 3),),
-        "ab0.0": ((0, 17, 0),),
-        "ab0.2": ((0, 6, 1),),
-        "ab1.1": ((0, 9, 1),),
-        "ab1.3": ((0, 7, 1),),
-        "ab2.3": ((0, 10, 1),),
-        "da1": ((0, 8, 1), (0, 9, 2),),
-        "ab3.0": ((0, 12, 0), (0, 13, 0), (0, 14, 0), (0, 15, 0), (0, 16, 0),),
-        "ab3.2": ((0, 9, 3), (0, 11, 1),),
-        "ab4.0": ((0, 10, 2),),
-        "ab4.3": ((0, 17, 1),),
-        "ab5.2": ((0, 6, 2), (0, 11, 2),),
-        "da2": ((0, 7, 2),),
-        "bp0": ((0, 12, 1), (0, 8, 2), (0, 13, 1),),
-        "bp1": ((0, 17, 2),),
-        "lnb1": ((0, 6, 3), (0, 14, 1), (0, 12, 2),),
-        "vs0": ((0, 7, 3), (0, 13, 2),),
-        "vs1": ((0, 8, 3), (0, 15, 1), (0, 14, 2),),
-        "out1": ((0, 12, 3),),
-        "fin": ((0, 10, 3), (0, 11, 3), (0, 13, 3), (0, 14, 3), (0, 15, 2), (0, 16, 1), (0, 17, 3),),
-        "end": ((0, 15, 3), (0, 16, 2), (0, 16, 3),),
+        "norm": ((1, 0, 0), (1, 5, 0), (1, 7, 0), (1, 10, 0), (1, 12, 0), (1, 15, 0), (1, 16, 0),),
+        "mask0": ((1, 1, 0),),
+        "mask2": ((1, 2, 0),),
+        "mask3": ((1, 0, 1),),
+        "stack1": ((1, 3, 0),),
+        "stack3": ((1, 1, 1),),
+        "proj0.0": ((1, 0, 2), (1, 4, 0), (1, 2, 1), (1, 5, 1), (1, 3, 1), (1, 1, 2), (1, 4, 1), (1, 6, 0), (1, 0, 3), (1, 2, 2), (1, 5, 2), (1, 7, 1), (1, 1, 3), (1, 3, 2), (1, 6, 1), (1, 8, 0), (1, 2, 3), (1, 5, 3), (1, 4, 2),),
+        "proj0.1": ((1, 9, 0),),
+        "att0.0": ((1, 7, 2),),
+        "att0.2": ((1, 3, 3), (1, 10, 1),),
+        "att1.0": ((1, 6, 2),),
+        "att1.2": ((1, 8, 1),),
+        "att2.1": ((1, 4, 3), (1, 9, 1), (1, 11, 0),),
+        "att2.3": ((1, 7, 3),),
+        "proj1.0": ((1, 12, 1),),
+        "proj1.1": ((1, 10, 2),),
+        "att3.3": ((1, 8, 2),),
+        "att4.0": ((1, 11, 1), (1, 13, 0),),
+        "att5.0": ((1, 6, 3), (1, 14, 0),),
+        "att5.1": ((1, 10, 3), (1, 12, 2),),
+        "att5.2": ((1, 9, 2),),
+        "att5.3": ((1, 15, 1),),
+        "ln2": ((1, 8, 3), (1, 11, 2), (1, 13, 1),),
+        "in0": ((1, 14, 1), (1, 16, 1), (1, 12, 3),),
+        "in1": ((1, 9, 3),),
+        "in2": ((1, 15, 2),),
+        "in3": ((1, 13, 2),),
+        "dc1": ((1, 11, 3),),
+        "dc2": ((1, 14, 2), (1, 16, 2),),
+        "bh0": ((1, 15, 3), (1, 13, 3), (0, 0, 0), (0, 2, 0), (1, 16, 3),),
+        "bh1": ((1, 14, 3), (0, 1, 0),),
+        "bh3": ((0, 0, 1),),
+        "bi1": ((0, 3, 0), (0, 4, 0),),
+        "db0": ((0, 1, 1), (0, 2, 1),),
+        "db2": ((0, 0, 2), (0, 8, 0),),
+        "db3": ((0, 4, 1),),
+        "go": ((0, 3, 1),),
+        "dwo": ((0, 0, 3),),
+        "ab0.0": ((0, 1, 2), (0, 5, 0), (0, 9, 0),),
+        "ab0.1": ((0, 2, 2),),
+        "ab1.0": ((0, 1, 3),),
+        "ab1.2": ((0, 4, 2), (0, 6, 0), (0, 10, 0),),
+        "ab1.3": ((0, 3, 2),),
+        "ab2.2": ((0, 5, 1),),
+        "ab2.3": ((0, 2, 3), (0, 4, 3), (0, 7, 0),),
+        "ab3.0": ((0, 3, 3), (0, 11, 0),),
+        "ab3.1": ((0, 6, 1),),
+        "ab3.3": ((0, 8, 1),),
+        "ab4.2": ((0, 9, 1),),
+        "ab4.3": ((0, 7, 1),),
+        "ab5.1": ((0, 10, 1),),
+        "ab5.3": ((0, 5, 2), (0, 12, 0),),
+        "da2": ((0, 15, 0),),
+        "da3": ((0, 8, 2),),
+        "bp1": ((0, 5, 3), (0, 9, 2),),
+        "lnb1": ((0, 6, 2), (0, 7, 2), (0, 10, 2), (0, 11, 1), (0, 13, 0),),
+        "vs0": ((0, 8, 3), (0, 15, 1),),
+        "vs1": ((0, 6, 3), (0, 7, 3), (0, 9, 3), (0, 12, 1), (0, 14, 0),),
+        "out1": ((0, 10, 3), (0, 11, 2),),
+        "fin": ((0, 13, 1),),
+        "vs2": ((0, 15, 2),),
+        "end": ((0, 12, 2), (0, 14, 1), (0, 15, 3), (0, 13, 2), (0, 11, 3), (0, 14, 2), (0, 12, 3), (0, 13, 3), (0, 14, 3),),
     },
 )
 
@@ -723,12 +722,14 @@
         [w_query[...], w_key[...], w_value[...], w_output[...].T], axis=1
     )
     G[1, 0, z, x] = w_in[...]
-    G[2, 0, z, x] = w_out[...].T
+    G[2, 0, z, x] = w_out[...]
     pl.semaphore_wait(barrier, len(partners))
     tick("norm")
 
-    gain_one, shift_one = gain_one[...], shift_one[...]
-    gain_two, shift_two = gain_two[...], shift_two[...]
+    gain_one, shift_one, gain_two, shift_two, bias_out = (
+        ref[...].reshape(1, features)
+        for ref in (gain_one, shift_one, gain_two, shift_two, bias_out)
+    )
     piece = 128
     pieces = rows // piece
 
@@ -951,7 +952,7 @@
         return (
             carry[0] + column_sum(grad * unit),
             carry[1] + column_sum(grad),
-            carry[2] + column_sum(coming * (middle + bias_out[...])),
+            carry[2] + column_sum(coming * (middle + bias_out)),
         )
 
     sums = lax.fori_loop(0, pieces, second_back, (zero_row,) * 3)
@@ -1116,7 +1117,7 @@
     tick("fin")
 
     def finish_block(i, carry):
-        value = R32[chunk(i), :] + SR[chunk(i), :] + XG[chunk(i), :].astype(F32) + bias_out[...]
+        value = R32[chunk(i), :] + SR[chunk(i), :] + XG[chunk(i), :].astype(F32) + bias_out
         layer_out[chunk(i), :] = (AVG[chunk(i), :] + depth[4] * value).astype(BF)
         return carry
 
@@ -1140,20 +1141,23 @@
         c.wait_send()
 
 
-def spread_body(width, cotangent, packed, sums, depth, stack, wq, wk, wv, wo, wi, wu, *rest):
+def spread_body(width, cotangent, average, tokens, packed, sums, depth, *outs):
+    layer_out, grad_tokens, stack, wq, wk, wv, wo, wi, wu = outs[:9]
+    gain_one, shift_one, gain_two, shift_two, bias_in, bias_out, grad_depth = outs[9:]
+    layer_out[...] = average[...]
+    grad_tokens[...] = tokens[...]
     for k in range(4):
         stack[k] = depth[k] * cotangent[...].astype(F32)
 
     @pl.when(pl.program_id(0) == 0)
     def _():
-        gain_one, shift_one, gain_two, shift_two, bias_in, bias_out, grad_depth = rest
         for n, ref in enumerate((wq, wk, wv)):
             ref[...] = packed[0, :, n * width : (n + 1) * width]
         wo[...] = packed[0, :, 3 * width :].T
         wi[...] = packed[1]
-        wu[...] = packed[2].T
+        wu[...] = packed[2]
         for n, ref in enumerate((gain_one, shift_one, gain_two, shift_two, bias_out)):
-            ref[...] = sums[n : n + 1, :]
+            ref[...] = sums[n, :]
         bias_in[...] = jnp.concatenate([sums[9 + n : 10 + n, :] for n in range(4)], axis=1)
         lane = lax.broadcasted_iota(jnp.int32, (1, 5), 1)
         total = jnp.zeros((1, 5), F32)
@@ -1242,9 +1246,6 @@
         dma((nz + 2,)),
     ]
 
-    def row(vector):
-        return vector.reshape(1, -1)
-
     layer_out, grad_tokens, packed, sums = pl.pallas_call(
         functools.partial(fused_body, nz, rows, features, shard, PLAN),
         out_shape=[
@@ -1268,45 +1269,48 @@
         w_value,
         w_output,
         w_in,
-        w_out,
-        row(gain_one),
-        row(shift_one),
-        row(gain_two),
-        row(shift_two),
-        row(bias_in),
-        row(bias_out),
+        w_out.T,
+        gain_one,
+        shift_one,
+        gain_two,
+        shift_two,
+        bias_in.reshape(1, -1),
+        bias_out,
         depth_weights,
         starts,
         jnp.asarray(cos_np.T.copy()),
         jnp.asarray(sin_np.T.copy()),
     )
 
-    part = rows // 4
+    steps = 4
+    part = rows // steps
     sizes = (
         [(shard, width)] * 3
-        + [(width, shard), (shard, features), (features, shard)]
-        + [(1, features)] * 4
-        + [(1, 4 * features), (1, features), (1, 5)]
+        + [(width, shard), (shard, features), (shard, features)]
+        + [(features,)] * 4
+        + [(1, 4 * features), (features,), (1, 5)]
     )
 
     def fixed(size):
         return pl.BlockSpec(size, lambda i: (0,) * len(size))
 
+    by_rows = pl.BlockSpec((part, features), lambda i: (i, 0))
     outs = pl.pallas_call(
         functools.partial(spread_body, width),
-        grid=(4,),
-        out_shape=[shape((4, rows, features), F32)] + [shape(size, F32) for size in sizes],
-        in_specs=[
-            pl.BlockSpec((part, features), lambda i: (i, 0)),
-            fixed((3, shard, features)),
-            fixed((16, features)),
-            smem,
-        ],
-        out_specs=[pl.BlockSpec((4, part, features), lambda i: (0, i, 0))]
+        grid=(steps,),
+        out_shape=[
+            shape((rows, features), BF),
+            shape((rows, features), F32),
+            shape((4, rows, features), F32),
+        ]
+        + [shape(size, F32) for size in sizes],
+        in_specs=[by_rows] * 3 + [fixed((3, shard, features)), fixed((16, features)), smem],
+        out_specs=[by_rows] * 2
+        + [pl.BlockSpec((4, part, features), lambda i: (0, i, 0))]
         + [fixed(size) for size in sizes],
-        compiler_params=pltpu.CompilerParams(vmem_limit_bytes=32 * 1024 * 1024),
-    )(cotangent, packed, sums, depth_weights)
-    return (layer_out, grad_tokens, *outs[:7], *[vector.reshape(-1) for vector in outs[7:]])
+        compiler_params=pltpu.CompilerParams(vmem_limit_bytes=60 * 1024 * 1024),
+    )(cotangent, layer_out, grad_tokens, packed, sums, depth_weights)
+    return (*outs[:8], outs[8].T, *outs[9:13], outs[13].reshape(-1), outs[14], outs[15].reshape(-1))
 
 
 def per_device(*arrays):

time: 191 us -> 156 us (0.82)
  Pallas kernels: 171 us -> 155 us
  local copies, waits for them, and re-layouts: 15.9 us -> 0 us
  other arithmetic: 3.03 us -> 0 us
    pallas_call x1, Pallas kernels: 167 us -> 148 us  [fused_device(): pl.pallas_call(functools.partial(fused_body, nz, rows, features, shard, P...]
    unnamed x14 -> x0, local copies, waits for them, and re-layouts: 9.55 us -> none
    reshape x5 -> x0, local copies, waits for them, and re-layouts: 6.33 us -> none  [row(): return vector.reshape(1, -1)]
    pallas_call x5 -> x0, other arithmetic: 3.03 us -> none  [fused_device(): pl.pallas_call(functools.partial(spread_body, width), grid=(4,), out_shap...]
    pallas_call x1, Pallas kernels: 4.05 us -> 6.88 us  [fused_device(): pl.pallas_call(functools.partial(spread_body, width), grid=(steps,), out_...]
where the time goes in v1:
time: 156 us
  Pallas kernels  155 us (99%)
    pallas_call x1, Pallas kernels, fused_device(): pl.pallas_call(functools.partial(fused_body, nz, rows, features, shard, P...  148 us
    pallas_call x1, Pallas kernels, fused_device(): pl.pallas_call(functools.partial(spread_body, width), grid=(steps,), out_...  6.88 us

profile of v1, /device:TPU:0, one launch (start us, length us, event | category | flops | bytes accessed | tf_op | source)
XLA Modules:
  0.0 155.9 jit_solution(9323500936805650483)
XLA Ops:
  0.7 148.2 %shard_map.306 = (bf16[512,768]{1,0:T(8,128)(2,1)}, f32[512,768]{1,0:T(8,128)}, f32[3,96,768]{2,1,0:T(8,128)}, f32[16,768]{1,0:T(8,128)}) custom-call(bf16[512,768]{1,0:T(8,128)(2,1)} %tokens_hbm.1, bf16[512,768]{1,0:T(8,128)(2,1)} %cotangent.1, bf16[4,512,768]{2,1,0:T(8,128)(2,1)} %stack.1, bf16[96,192]{1,0:T(8,128)(2,1)} %w_query.1, ...), custom_call_target="tpu_custom_call" | custom-call | tf_op jit(solution)/shard_map/pallas_call | solution.py:1249
  148.9 6.9 %shard_map.307 = (bf16[512,768]{1,0:T(8,128)(2,1)}, f32[512,768]{1,0:T(8,128)}, f32[4,512,768]{2,1,0:T(8,128)}, f32[96,192]{1,0:T(8,128)}, f32[96,192]{1,0:T(8,1...) custom-call(bf16[512,768]{1,0:T(8,128)(2,1)} %cotangent.1, ...), custom_call_target="tpu_custom_call" | custom-call | tf_op jit(solution)/shard_map/pallas_call | solution.py:1298

commit v2 on v1

--- a/solution.py
+++ b/solution.py
@@ -314,98 +314,96 @@
         ("A", 0, 512, 128),
         ("B", 0, 640, 128),
         ("A", 1, 0, 256),
-        ("B", 1, 256, 128),
-        ("A", 1, 384, 128),
-        ("A", 1, 512, 128),
+        ("A", 1, 256, 256),
+        ("B", 1, 512, 128),
         ("B", 1, 640, 128),
-        ("A", 2, 0, 128),
-        ("B", 2, 128, 128),
-        ("A", 2, 256, 128),
+        ("A", 2, 0, 256),
+        ("B", 2, 256, 128),
         ("A", 2, 384, 128),
         ("B", 2, 512, 128),
         ("B", 2, 640, 128),
     ),
     (
-        ("B", 2, 0, 128),
-        ("B", 2, 128, 128),
-        ("A", 2, 256, 256),
-        ("A", 2, 512, 128),
+        ("A", 2, 0, 256),
+        ("B", 2, 256, 128),
+        ("A", 2, 384, 256),
         ("B", 2, 640, 128),
         ("B", 1, 0, 128),
-        ("B", 1, 128, 128),
+        ("A", 1, 128, 128),
         ("B", 1, 256, 128),
-        ("A", 1, 384, 128),
-        ("A", 1, 512, 128),
-        ("A", 1, 640, 128),
-        ("A", 0, 0, 256),
+        ("A", 1, 384, 256),
+        ("B", 1, 640, 128),
+        ("A", 0, 0, 128),
+        ("A", 0, 128, 128),
         ("A", 0, 256, 128),
         ("A", 0, 384, 128),
         ("A", 0, 512, 128),
         ("B", 0, 640, 128),
     ),
     {
-        "norm": ((1, 0, 0), (1, 5, 0), (1, 7, 0), (1, 10, 0), (1, 12, 0), (1, 15, 0), (1, 16, 0),),
-        "mask0": ((1, 1, 0),),
+        "norm": ((1, 0, 0), (1, 5, 0), (1, 8, 0), (1, 9, 0),),
+        "mask0": ((1, 1, 0), (1, 11, 0), (1, 13, 0), (1, 14, 0),),
         "mask2": ((1, 2, 0),),
         "mask3": ((1, 0, 1),),
-        "stack1": ((1, 3, 0),),
+        "stack2": ((1, 3, 0),),
         "stack3": ((1, 1, 1),),
-        "proj0.0": ((1, 0, 2), (1, 4, 0), (1, 2, 1), (1, 5, 1), (1, 3, 1), (1, 1, 2), (1, 4, 1), (1, 6, 0), (1, 0, 3), (1, 2, 2), (1, 5, 2), (1, 7, 1), (1, 1, 3), (1, 3, 2), (1, 6, 1), (1, 8, 0), (1, 2, 3), (1, 5, 3), (1, 4, 2),),
-        "proj0.1": ((1, 9, 0),),
-        "att0.0": ((1, 7, 2),),
-        "att0.2": ((1, 3, 3), (1, 10, 1),),
-        "att1.0": ((1, 6, 2),),
-        "att1.2": ((1, 8, 1),),
-        "att2.1": ((1, 4, 3), (1, 9, 1), (1, 11, 0),),
-        "att2.3": ((1, 7, 3),),
-        "proj1.0": ((1, 12, 1),),
-        "proj1.1": ((1, 10, 2),),
-        "att3.3": ((1, 8, 2),),
-        "att4.0": ((1, 11, 1), (1, 13, 0),),
-        "att5.0": ((1, 6, 3), (1, 14, 0),),
-        "att5.1": ((1, 10, 3), (1, 12, 2),),
-        "att5.2": ((1, 9, 2),),
-        "att5.3": ((1, 15, 1),),
-        "ln2": ((1, 8, 3), (1, 11, 2), (1, 13, 1),),
-        "in0": ((1, 14, 1), (1, 16, 1), (1, 12, 3),),
-        "in1": ((1, 9, 3),),
-        "in2": ((1, 15, 2),),
-        "in3": ((1, 13, 2),),
-        "dc1": ((1, 11, 3),),
-        "dc2": ((1, 14, 2), (1, 16, 2),),
-        "bh0": ((1, 15, 3), (1, 13, 3), (0, 0, 0), (0, 2, 0), (1, 16, 3),),
-        "bh1": ((1, 14, 3), (0, 1, 0),),
-        "bh3": ((0, 0, 1),),
-        "bi1": ((0, 3, 0), (0, 4, 0),),
-        "db0": ((0, 1, 1), (0, 2, 1),),
-        "db2": ((0, 0, 2), (0, 8, 0),),
-        "db3": ((0, 4, 1),),
-        "go": ((0, 3, 1),),
-        "dwo": ((0, 0, 3),),
-        "ab0.0": ((0, 1, 2), (0, 5, 0), (0, 9, 0),),
-        "ab0.1": ((0, 2, 2),),
-        "ab1.0": ((0, 1, 3),),
-        "ab1.2": ((0, 4, 2), (0, 6, 0), (0, 10, 0),),
-        "ab1.3": ((0, 3, 2),),
-        "ab2.2": ((0, 5, 1),),
-        "ab2.3": ((0, 2, 3), (0, 4, 3), (0, 7, 0),),
-        "ab3.0": ((0, 3, 3), (0, 11, 0),),
-        "ab3.1": ((0, 6, 1),),
-        "ab3.3": ((0, 8, 1),),
-        "ab4.2": ((0, 9, 1),),
-        "ab4.3": ((0, 7, 1),),
-        "ab5.1": ((0, 10, 1),),
-        "ab5.3": ((0, 5, 2), (0, 12, 0),),
-        "da2": ((0, 15, 0),),
+        "proj0.0": ((1, 4, 0), (1, 0, 2), (1, 2, 1), (1, 5, 1), (1, 1, 2), (1, 3, 1), (1, 4, 1), (1, 0, 3), (1, 6, 0), (1, 2, 2), (1, 5, 2), (1, 1, 3), (1, 7, 0), (1, 3, 2), (1, 6, 1), (1, 2, 3), (1, 8, 1), (1, 5, 3), (1, 4, 2),),
+        "att0.0": ((1, 7, 1),),
+        "att0.1": ((1, 3, 3),),
+        "att0.2": ((1, 9, 1),),
+        "att0.3": ((1, 6, 2),),
+        "att2.0": ((1, 8, 2),),
+        "att2.2": ((1, 4, 3), (1, 10, 0),),
+        "att3.0": ((1, 9, 2),),
+        "att3.2": ((1, 11, 1),),
+        "att3.3": ((1, 7, 2), (1, 8, 3),),
+        "att5.0": ((1, 10, 1),),
+        "att5.2": ((1, 6, 3), (1, 12, 0),),
+        "r.other": ((1, 9, 3),),
+        "r.low": ((1, 13, 1),),
+        "ln2": ((1, 11, 2),),
+        "in0": ((1, 10, 2), (1, 14, 1),),
+        "in1": ((1, 12, 1), (1, 7, 3),),
+        "in3": ((1, 11, 3), (1, 13, 2),),
+        "dc2": ((1, 14, 2),),
+        "dc3": ((1, 12, 2),),
+        "bh0": ((1, 13, 3), (1, 10, 3), (0, 1, 0), (0, 0, 0), (1, 14, 3),),
+        "bh1": ((1, 12, 3), (0, 3, 0),),
+        "bh2": ((0, 1, 1),),
+        "bh3": ((0, 2, 0),),
+        "lnb2": ((0, 0, 1), (0, 3, 1),),
+        "db3": ((0, 1, 2),),
+        "go": ((0, 4, 0), (0, 5, 0),),
+        "dwo": ((0, 0, 2),),
+        "ab0.0": ((0, 1, 3), (0, 2, 1),),
+        "ab0.1": ((0, 3, 2),),
+        "ab0.2": ((0, 7, 0),),
+        "ab1.0": ((0, 4, 1),),
+        "ab1.1": ((0, 3, 3), (0, 0, 3), (0, 5, 1),),
+        "ab1.3": ((0, 6, 0),),
+        "ab2.0": ((0, 2, 2),),
+        "ab2.3": ((0, 4, 2),),
+        "da0": ((0, 5, 2), (0, 8, 0),),
+        "ab3.0": ((0, 9, 0),),
+        "ab3.1": ((0, 4, 3), (0, 6, 1),),
+        "ab3.2": ((0, 2, 3), (0, 7, 1),),
+        "ab3.3": ((0, 10, 0),),
+        "ab4.0": ((0, 5, 3),),
+        "ab4.2": ((0, 8, 1),),
+        "ab4.3": ((0, 14, 0),),
+        "ab5.0": ((0, 6, 2), (0, 11, 0),),
+        "ab5.3": ((0, 7, 2),),
+        "da2": ((0, 6, 3),),
         "da3": ((0, 8, 2),),
-        "bp1": ((0, 5, 3), (0, 9, 2),),
-        "lnb1": ((0, 6, 2), (0, 7, 2), (0, 10, 2), (0, 11, 1), (0, 13, 0),),
-        "vs0": ((0, 8, 3), (0, 15, 1),),
-        "vs1": ((0, 6, 3), (0, 7, 3), (0, 9, 3), (0, 12, 1), (0, 14, 0),),
-        "out1": ((0, 10, 3), (0, 11, 2),),
-        "fin": ((0, 13, 1),),
-        "vs2": ((0, 15, 2),),
-        "end": ((0, 12, 2), (0, 14, 1), (0, 15, 3), (0, 13, 2), (0, 11, 3), (0, 14, 2), (0, 12, 3), (0, 13, 3), (0, 14, 3),),
+        "bp0": ((0, 9, 1), (0, 12, 0),),
+        "bp1": ((0, 10, 1), (0, 14, 1),),
+        "lnb1": ((0, 7, 3), (0, 8, 3), (0, 9, 2), (0, 11, 1), (0, 13, 0),),
+        "vs0": ((0, 10, 2), (0, 12, 1), (0, 14, 2),),
+        "vs1": ((0, 9, 3), (0, 11, 2), (0, 13, 1),),
+        "out1": ((0, 10, 3), (0, 12, 2), (0, 14, 3),),
+        "fin": ((0, 11, 3), (0, 13, 2),),
+        "vs2": ((0, 12, 3),),
+        "end": ((0, 13, 3),),
     },
 )
 
@@ -474,8 +472,8 @@
     starts,
     cosine_t,
     sine_t,
-    layer_out,
-    grad_tokens,
+    layer_hbm,
+    grad_tokens_hbm,
     grad_packed,
     grad_vectors,
     G,
@@ -501,7 +499,6 @@
     R32,
     AVG,
     SR,
-    XR,
     SB,
     XG,
     VS,
@@ -514,6 +511,7 @@
     cosine,
     sine,
     BI,
+    grad_tokens,
     local_sem,
     ag_send,
     ag_recv,
@@ -586,11 +584,13 @@
                 for copy in gather_copies(f, past)[0]:
                     copy().wait_send()
             return
-        if stage > 0:
-            for copy in gather_copies(f, stage - 1)[1]:
+        awaited = {1: 0, 2: 1, 3: 2, 5: 1}.get(stage)
+        if awaited is not None:
+            for copy in gather_copies(f, awaited)[1]:
                 copy().wait_recv()
-        if stage < 3:
-            for copy in gather_copies(f, stage)[0]:
+        started = {0: 0, 1: 1, 2: 2, 6: 2}.get(stage)
+        if started is not None:
+            for copy in gather_copies(f, started)[0]:
                 copy().start()
 
     def reduce_copies(f, stage):
@@ -675,6 +675,11 @@
         for copy in after:
             copy().start()
 
+    def drain(k):
+        for f in range(len(gathers)):
+            if gathers[f][1] == k:
+                gather_step(f, 4)
+
     def tick(name):
         for gather, flow, stage in schedule.get(name, ()):
             if gather:
@@ -698,7 +703,11 @@
     take_a = sib_copy(0, A.at[low], A.at[other])
     send_gm = sib_copy(1, GM.at[low], GM.at[low])
     take_gm = sib_copy(1, GM.at[low], GM.at[other])
-    part_r = sib_copy(2, SR, XR)
+    half_rows = rows // 2
+    part_r = [
+        sib_copy(n, SB.at[pl.ds(i * half_rows, half_rows)], XG.at[pl.ds(i * half_rows, half_rows)])
+        for i, n in enumerate((2, 8))
+    ]
     send_c = sib_copy(3, C.at[low], C.at[low])
     take_c = sib_copy(3, C.at[low], C.at[other])
     part_g = sib_copy(4, SB, XG)
@@ -734,7 +743,12 @@
     pieces = rows // piece
 
     def chunk(i):
-        return pl.ds(pl.multiple_of(i * piece, piece), piece)
+        return pl.ds(i * piece if isinstance(i, int) else pl.multiple_of(i * piece, piece), piece)
+
+    def over_pieces(step, carry):
+        for i in range(pieces):
+            carry = step(i, carry)
+        return carry
 
     loads[0].wait()
     loads[1].wait()
@@ -821,17 +835,27 @@
                 at = 2 * width + h * HEAD_DIM
                 V[n, span, :HEAD_DIM] = result[:, at : at + HEAD_DIM].astype(BF)
 
+    def span_of(block):
+        lo = block * BLOCK
+        return lo, min(lo + 2 * BLOCK, length)
+
     def attend(n, carry):
         @pl.when(lax.rem(n, heads) == 0)
         def _():
             project(n // heads)
 
+        def scores(block):
+            lo, top = span_of(block)
+            return dot(K[n, 0:top, :], QT[n, :, lo : lo + BLOCK], 1, 0)
+
+        ahead = scores(0)
         for block in range(blocks):
             tick_at("att", n, 2 * heads, "." + str(block))
-            lo = block * BLOCK
-            top = min(lo + 2 * BLOCK, length)
+            lo, top = span_of(block)
             half, at = lo // rows, lo % rows
-            score = dot(K[n, 0:top, :], QT[n, :, lo : lo + BLOCK], 1, 0) * EXPONENT_SCALE
+            score = ahead * EXPONENT_SCALE
+            if block + 1 < blocks:
+                ahead = scores(block + 1)
             tail = score[lo:] + MB[block, 0 : top - lo, :]
             score = jnp.concatenate([score[:lo], tail], axis=0) if lo else tail
             highest = jnp.max(score, axis=0, keepdims=True)
@@ -839,7 +863,7 @@
             mixed = dot(V[n, 0:top, :], power, 0, 0)
             total = mixed[HEAD_DIM : HEAD_DIM + 1, :]
             OT[half, n, :, at : at + BLOCK] = (mixed[:HEAD_DIM, :] / total).astype(BF)
-            LS[n, :, lo : lo + BLOCK] = highest + jnp.log2(total)
+            LS[pl.ds(n, 1), lo : lo + BLOCK] = highest + jnp.log2(total)
         return carry
 
     lax.fori_loop(0, 2 * heads, attend, 0)
@@ -852,21 +876,25 @@
         return OT[half].reshape(2 * width, rows)
 
     tick("r.other")
-    SR[...] = dot(mixed_rows(other), WO[...], 0, 0)
-    part_r.start()
+    for i in range(2):
+        span = slice(i * half_rows, (i + 1) * half_rows)
+        left = OT[other, :, :, span].reshape(2 * width, half_rows)
+        SB[span, :] = dot(left, WO[...], 0, 0).astype(BF)
+        part_r[i].start()
     tick("r.low")
     R32[...] = dot(mixed_rows(low), WO[...], 0, 0)
-    part_r.wait_recv()
+    for copy in part_r:
+        copy.wait_recv()
     tick("ln2")
 
     def second_norm(i, carry):
-        middle = tokens[chunk(i), :].astype(F32) + R32[chunk(i), :] + XR[chunk(i), :]
+        middle = tokens[chunk(i), :].astype(F32) + R32[chunk(i), :] + XG[chunk(i), :].astype(F32)
         R32[chunk(i), :] = middle
         unit, _ = norm_parts(middle)
         C[low, chunk(i), :] = (unit * gain_two + shift_two).astype(BF)
         return carry
 
-    lax.fori_loop(0, pieces, second_norm, 0)
+    over_pieces(second_norm, 0)
     send_c.start()
     def hidden_bias(slot):
         return BI[pl.ds(lax.rem(t + 2 * slot, 4), 1), :]
@@ -889,14 +917,14 @@
     take_gm.wait_recv()
 
     def outer_products(name, k, left, right):
-        half_rows = features // 2
+        half_cols = features // 2
 
         def one(i, carry):
             tick_at(name, i, 4)
             slot, part = 1 - i // 2, lax.rem(i, 2)
-            cols = pl.ds(pl.multiple_of(part * half_rows, 128), half_rows)
+            cols = pl.ds(pl.multiple_of(part * half_cols, 128), half_cols)
             value = dot(
-                left[:, :, cols].reshape(length, half_rows),
+                left[:, :, cols].reshape(length, half_cols),
                 right[pl.ds(2 * slot, 2)].reshape(length, features),
                 0,
                 0,
@@ -931,11 +959,14 @@
 
         @pl.when(i == 0)
         def _():
+            for copy in part_r:
+                copy.wait_send()
             SB[...] = grad_tokens[...].astype(BF)
             part_g.start()
 
         return carry
 
+    drain(0)
     VS[13:14, :] = lax.fori_loop(0, 2, back, zero_row) / depth[4]
     part_g.wait_recv()
     send_gm.wait_send()
@@ -962,6 +993,7 @@
     VS[13:14, :] = VS[13:14, :] + sums[2]
     outer_products("db", 1, C, GP)
 
+    drain(1)
     take_gl.wait_recv()
     tick("go")
 
@@ -995,27 +1027,39 @@
         def place(which):
             return pl.ds(pl.multiple_of(which * width + h * HEAD_DIM, HEAD_DIM), HEAD_DIM)
 
-        GKA[...] = jnp.zeros_like(GKA)
-        GVA[...] = jnp.zeros_like(GVA)
-        for block in range(blocks):
-            tick_at("ab", i, 2 * heads, "." + str(block))
-            lo = block * BLOCK
-            top = min(lo + 2 * BLOCK, length)
+        def products(block):
+            lo, top = span_of(block)
+            half, at = lo // rows, lo % rows
+            grad_t = GOT[half, n, :, at : at + BLOCK]
+            return (
+                dot(K[n, 0:top, :], QT[n, :, lo : lo + BLOCK], 1, 0),
+                dot(V[n, 0:top, :HEAD_DIM], grad_t, 1, 0),
+            )
+
+        for step in range(blocks):
+            tick_at("ab", i, 2 * heads, "." + str(step))
+            block = blocks - 1 - step
+            lo, top = span_of(block)
             half, at = lo // rows, lo % rows
             here = slice(at, at + BLOCK)
+            score, grad_power = products(block)
             grad_t = GOT[half, n, :, here]
             delta = jnp.sum(
                 OT[half, n, :, here].astype(F32) * grad_t.astype(F32), axis=0, keepdims=True
             )
-            score = dot(K[n, 0:top, :], QT[n, :, lo : lo + BLOCK], 1, 0) * EXPONENT_SCALE
-            score = score - LS[n, :, lo : lo + BLOCK]
+            score = score * EXPONENT_SCALE - LS[pl.ds(n, 1), lo : lo + BLOCK]
             tail = score[lo:] + MB[block, 0 : top - lo, :]
             score = jnp.concatenate([score[:lo], tail], axis=0) if lo else tail
             power = jnp.exp2(score)
-            grad_power = dot(V[n, 0:top, :HEAD_DIM], grad_t, 1, 0)
             grad_score = (power * (grad_power - delta)).astype(BF)
-            GVA[:, 0:top] += dot(grad_t, power.astype(BF), 1, 1)
-            GKA[:, 0:top] += dot(QT[n, :, lo : lo + BLOCK], grad_score, 1, 1)
+            grad_value = dot(grad_t, power.astype(BF), 1, 1)
+            grad_key = dot(QT[n, :, lo : lo + BLOCK], grad_score, 1, 1)
+            if step:
+                GVA[:, 0:top] += grad_value
+                GKA[:, 0:top] += grad_key
+            else:
+                GVA[...] = grad_value
+                GKA[...] = grad_key
             grad_query = dot(KT[n, :, 0:top], grad_score, 1, 0) * scale
             GT[slot, half, place(0), here] = unturn(grad_query, slice(lo, lo + BLOCK)).astype(BF)
         for half in range(2):
@@ -1027,8 +1071,8 @@
         def _():
             for part in range(2):
                 tick_at("da", 2 * (1 - slot) + part, 4)
-                half_rows = features // 2
-                cols = slice(part * half_rows, (part + 1) * half_rows)
+                half_cols = features // 2
+                cols = slice(part * half_cols, (part + 1) * half_cols)
                 value = dot(A[0, :, cols], GT[slot, 0], 0, 1) + dot(
                     A[1, :, cols], GT[slot, 1], 0, 1
                 )
@@ -1045,7 +1089,6 @@
         return sum(dot(GT[s, half], whole(G, 0, s)[:, : 3 * width], 0, 1) for s in range(2))
 
     part_g.wait_send()
-    part_r.wait_send()
 
     def back_projects(i, carry):
         tick_at("bp", i, 2)
@@ -1068,7 +1111,9 @@
         grad_tokens[chunk(i), :] = grad_tokens[chunk(i), :] + norm_back(grad, gain_one, unit, inverse)
         return (carry[0] + column_sum(grad * unit), carry[1] + column_sum(grad))
 
-    sums = lax.fori_loop(0, pieces, first_back, (zero_row, zero_row))
+    sums = over_pieces(first_back, (zero_row, zero_row))
+    store_tokens = pltpu.make_async_copy(grad_tokens, grad_tokens_hbm, local_sem.at[3])
+    store_tokens.start()
     VS[0:1, :] = sums[0]
     VS[1:2, :] = sums[1]
 
@@ -1118,10 +1163,12 @@
 
     def finish_block(i, carry):
         value = R32[chunk(i), :] + SR[chunk(i), :] + XG[chunk(i), :].astype(F32) + bias_out
-        layer_out[chunk(i), :] = (AVG[chunk(i), :] + depth[4] * value).astype(BF)
+        tokens[chunk(i), :] = (AVG[chunk(i), :] + depth[4] * value).astype(BF)
         return carry
 
     lax.fori_loop(0, pieces, finish_block, 0)
+    store_layer = pltpu.make_async_copy(tokens, layer_hbm, local_sem.at[4])
+    store_layer.start()
     tick("vs2")
     for j in range(nz - 1):
         remote(
@@ -1132,11 +1179,12 @@
     for j in range(1, nz):
         total = total + VZ[j]
     grad_vectors[...] = total
-    for f in range(len(gathers)):
-        gather_step(f, 4)
+    drain(2)
     tick("end")
     for f in range(len(reduces)):
         reduce_step(f, 4)
+    store_tokens.wait()
+    store_layer.wait()
     for c in [send_a, send_c, send_gl, part_b, round_s, round_y, round_x] + rounds_z:
         c.wait_send()
 
@@ -1212,14 +1260,13 @@
         pltpu.VMEM((2 * heads, HEAD_DIM, length), BF),
         pltpu.VMEM((2 * heads, HEAD_DIM, length), BF),
         pltpu.VMEM((2, 2 * heads, HEAD_DIM, rows), BF),
-        pltpu.VMEM((2 * heads, 1, length), F32),
+        pltpu.VMEM((8, length), F32),
         pltpu.VMEM((length // BLOCK, 2 * BLOCK, BLOCK), F32),
         pltpu.VMEM((4, rows, features), BF),
         pltpu.VMEM((4, rows, features), BF),
         pltpu.VMEM((2, 2 * heads, HEAD_DIM, rows), BF),
         pltpu.VMEM((2, 2, 3 * width, rows), BF),
         pltpu.VMEM((2 * width, features), BF),
-        pltpu.VMEM((rows, features), F32),
         pltpu.VMEM((rows, features), F32),
         pltpu.VMEM((rows, features), F32),
         pltpu.VMEM((rows, features), F32),
@@ -1235,13 +1282,14 @@
         pltpu.VMEM((length, 2 * HEAD_DIM), F32),
         pltpu.VMEM((length, 2 * HEAD_DIM), F32),
         pltpu.VMEM((4, features), F32),
-        dma((3,)),
+        pltpu.VMEM((rows, features), F32),
+        dma((5,)),
         dma((len(gathers), nz + 1)),
         dma((len(gathers), nz + 1)),
         dma((len(reduces), nz + 2)),
         dma((len(reduces), nz + 2)),
-        dma((8,)),
-        dma((8,)),
+        dma((9,)),
+        dma((9,)),
         dma((nz + 2,)),
         dma((nz + 2,)),
     ]
@@ -1255,7 +1303,7 @@
             shape((16, features), F32),
         ],
         in_specs=[hbm] * 3 + [vmem] * 12 + [smem] * 2 + [vmem] * 2,
-        out_specs=[vmem] * 4,
+        out_specs=[hbm] * 2 + [vmem] * 2,
         scratch_shapes=scratch,
         compiler_params=pltpu.CompilerParams(
             collective_id=0, has_side_effects=True, vmem_limit_bytes=64 * 1024 * 1024
@@ -1282,7 +1330,7 @@
         jnp.asarray(sin_np.T.copy()),
     )
 
-    steps = 4
+    steps = 2
     part = rows // steps
     sizes = (
         [(shard, width)] * 3

time: 156 us -> 148 us (0.949)
  Pallas kernels: 155 us -> 147 us
    pallas_call x1, Pallas kernels: 148 us -> 141 us  [fused_device(): pl.pallas_call(functools.partial(fused_body, nz, rows, features, shard, P...]
where the time goes in v2:
time: 148 us
  Pallas kernels  147 us (99%)
    pallas_call x1, Pallas kernels, fused_device(): pl.pallas_call(functools.partial(fused_body, nz, rows, features, shard, P...  141 us
    pallas_call x1, Pallas kernels, fused_device(): pl.pallas_call(functools.partial(spread_body, width), grid=(steps,), out_...  6.06 us

profile of v2, /device:TPU:0, one launch (start us, length us, event | category | flops | bytes accessed | tf_op | source)
XLA Modules:
  0.0 148.3 jit_solution(7246281571056416950)
XLA Ops:
  0.7 141.4 %shard_map.306 = (bf16[512,768]{1,0:T(8,128)(2,1)}, f32[512,768]{1,0:T(8,128)}, f32[3,96,768]{2,1,0:T(8,128)}, f32[16,768]{1,0:T(8,128)}) custom-call(bf16[512,768]{1,0:T(8,128)(2,1)} %tokens_hbm.1, bf16[512,768]{1,0:T(8,128)(2,1)} %cotangent.1, bf16[4,512,768]{2,1,0:T(8,128)(2,1)} %stack.1, bf16[96,192]{1,0:T(8,128)(2,1)} %w_query.1, ...), custom_call_target="tpu_custom_call" | custom-call | tf_op jit(solution)/shard_map/pallas_call | solution.py:1297
  142.1 6.1 %shard_map.307 = (bf16[512,768]{1,0:T(8,128)(2,1)}, f32[512,768]{1,0:T(8,128)}, f32[4,512,768]{2,1,0:T(8,128)}, f32[96,192]{1,0:T(8,128)}, f32[96,192]{1,0:T(8,1...) custom-call(bf16[512,768]{1,0:T(8,128)(2,1)} %cotangent.1, ...), custom_call_target="tpu_custom_call" | custom-call | tf_op jit(solution)/shard_map/pallas_call | solution.py:1346

commit v3 on v2

--- a/solution.py
+++ b/solution.py
@@ -502,8 +502,12 @@
     SB,
     XG,
     VS,
-    VR,
-    VZ,
+    V8,
+    VI,
+    VP,
+    VO,
+    VL,
+    VM,
     GKA,
     GVA,
     tokens,
@@ -521,6 +525,8 @@
     sib_recv,
     vec_send,
     vec_recv,
+    late_send,
+    late_recv,
 ):
     length = 2 * rows
     heads = 3
@@ -539,6 +545,20 @@
 
     def zpeer(j):
         return (lax.rem(z + j, nz) * 2 + x, t)
+
+    def near_place(j):
+        side = x + (1 - 2 * x) * (j // 4)
+        upper = pair + (1 - 2 * pair) * ((j // 2) % 2)
+        lower = low + (1 - 2 * low) * (j % 2)
+        return side, 2 * upper + lower
+
+    def near(j):
+        side, place = near_place(j)
+        return 2 * z + side, place
+
+    def near_slot(j):
+        side, place = near_place(j)
+        return 4 * side + place
 
     def remote(src, dst, send, recv, peer):
         return pltpu.make_async_remote_copy(
@@ -724,7 +744,7 @@
     for load in loads:
         load.start()
     barrier = pltpu.get_barrier_semaphore()
-    partners = [sib, ypeer, xpeer] + [zpeer(j + 1) for j in range(nz - 1)]
+    partners = [near(j) for j in range(1, 8)] + [zpeer(j + 1) for j in range(nz - 1)]
     for peer in partners:
         pl.semaphore_signal(barrier, inc=1, device_id=peer, device_id_type=MESH)
     G[0, 0, z, x] = jnp.concatenate(
@@ -991,6 +1011,60 @@
     VS[3:4, :] = sums[1]
     send_gl.start()
     VS[13:14, :] = VS[13:14, :] + sums[2]
+
+    def vector_step(step):
+        mine = near_slot(0)
+
+        def hop(kind, j):
+            if kind == 1:
+                source, target, peer, sem = VP.at[z], VP.at[z], zpeer(j), 6 + j
+            else:
+                source = V8.at[near_slot(j)] if kind == 0 else VO.at[mine]
+                target = VI.at[mine] if kind == 0 else VO.at[mine]
+                peer, sem = near(j), j - 1 + (nz + 6) * (kind // 2)
+            return remote(source, target, vec_send.at[sem], vec_recv.at[sem], peer)
+
+        def taken(kind, j):
+            if kind == 1:
+                target, sem = VP.at[lax.rem(z + nz - j, nz)], 6 + j
+            else:
+                target = (VI if kind == 0 else VO).at[near_slot(j)]
+                sem = j - 1 + (nz + 6) * (kind // 2)
+            peer = zpeer(j) if kind == 1 else near(j)
+            remote(V8.at[0], target, vec_send.at[sem], vec_recv.at[sem], peer).wait_recv()
+
+        def ends(kind):
+            return range(1, nz if kind == 1 else 8)
+
+        if step == 0:
+            for n in range(8):
+                V8[n] = VS[2 * n : 2 * n + 2, :]
+            VI[mine] = V8[mine]
+        elif step < 4:
+            for j in ends(step - 1):
+                taken(step - 1, j)
+            if step == 1:
+                total = VI[0]
+                for n in range(1, 8):
+                    total = total + VI[n]
+                VP[z] = total
+            elif step == 2:
+                total = VP[0]
+                for n in range(1, nz):
+                    total = total + VP[n]
+                VO[mine] = total
+            else:
+                for n in range(8):
+                    grad_vectors[2 * n : 2 * n + 2, :] = VO[n]
+        else:
+            for kind in range(3):
+                for j in ends(kind):
+                    hop(kind, j).wait_send()
+        if step < 3:
+            for j in ends(step):
+                hop(step, j).start()
+
+    vector_step(0)
     outer_products("db", 1, C, GP)
 
     drain(1)
@@ -1038,6 +1112,9 @@
 
         for step in range(blocks):
             tick_at("ab", i, 2 * heads, "." + str(step))
+            if step == 3:
+                pl.when(i == 1)(functools.partial(vector_step, 1))
+                pl.when(i == 4)(functools.partial(vector_step, 2))
             block = blocks - 1 - step
             lo, top = span_of(block)
             half, at = lo // rows, lo % rows
@@ -1114,19 +1191,25 @@
     sums = over_pieces(first_back, (zero_row, zero_row))
     store_tokens = pltpu.make_async_copy(grad_tokens, grad_tokens_hbm, local_sem.at[3])
     store_tokens.start()
-    VS[0:1, :] = sums[0]
-    VS[1:2, :] = sums[1]
-
-    def vector_round(n, src, peer):
-        copy = remote(src, VR.at[n], vec_send.at[n], vec_recv.at[n], peer)
-        copy.start()
-        return copy
-
-    round_s = vector_round(0, VS, sib)
+    VL[near_slot(0), 0:1, :] = sums[0]
+    VL[near_slot(0), 1:2, :] = sums[1]
+    late = [
+        remote(
+            VL.at[near_slot(0)], VL.at[near_slot(0)],
+            late_send.at[j - 1], late_recv.at[j - 1], near(j),
+        )
+        for j in range(1, 8)
+    ]
+    for c in late:
+        c.start()
+
+    def late_taken(j):
+        return remote(
+            VL.at[near_slot(0)], VL.at[near_slot(j)],
+            late_send.at[j - 1], late_recv.at[j - 1], near(j),
+        )
+
     tick("vs0")
-    round_s.wait_recv()
-    VZ[nz] = VS[...] + VR[0]
-    round_y = vector_round(1, VZ.at[nz], ypeer)
     tick("vs1")
 
     part_a.wait_send()
@@ -1141,23 +1224,25 @@
         @pl.when(i == 0)
         def _():
             SB[...] = SR[...].astype(BF)
+            late_taken(1).wait_recv()
             part_b.start()
 
         return carry
 
     lax.fori_loop(0, 1, outers, 0)
-    round_y.wait_recv()
-    VZ[nz + 1] = VZ[nz] + VR[1]
-    round_x = vector_round(2, VZ.at[nz + 1], xpeer)
     lax.fori_loop(1, 2, outers, 0)
     part_b.wait_recv()
-    round_x.wait_recv()
-    VZ[z] = VZ[nz + 1] + VR[2]
-    rounds_z = [
-        remote(VZ.at[z], VZ.at[z], vec_send.at[3 + j], vec_recv.at[3 + j], zpeer(j + 1))
+    for j in range(2, 8):
+        late_taken(j).wait_recv()
+    eight = VL[0]
+    for n in range(1, 8):
+        eight = eight + VL[n]
+    VM[z] = eight
+    last = [
+        remote(VM.at[z], VM.at[z], late_send.at[7 + j], late_recv.at[7 + j], zpeer(j + 1))
         for j in range(nz - 1)
     ]
-    for c in rounds_z:
+    for c in last:
         c.start()
     tick("fin")
 
@@ -1170,22 +1255,24 @@
     store_layer = pltpu.make_async_copy(tokens, layer_hbm, local_sem.at[4])
     store_layer.start()
     tick("vs2")
+    drain(2)
+    tick("end")
     for j in range(nz - 1):
         remote(
-            VZ.at[z], VZ.at[lax.rem(z + nz - 1 - j, nz)],
-            vec_send.at[3 + j], vec_recv.at[3 + j], zpeer(j + 1),
+            VM.at[z], VM.at[lax.rem(z + nz - 1 - j, nz)],
+            late_send.at[7 + j], late_recv.at[7 + j], zpeer(j + 1),
         ).wait_recv()
-    total = VZ[0]
+    first_sums = VM[0]
     for j in range(1, nz):
-        total = total + VZ[j]
-    grad_vectors[...] = total
-    drain(2)
-    tick("end")
+        first_sums = first_sums + VM[j]
+    vector_step(3)
+    grad_vectors[0:2, :] = first_sums
     for f in range(len(reduces)):
         reduce_step(f, 4)
     store_tokens.wait()
     store_layer.wait()
-    for c in [send_a, send_c, send_gl, part_b, round_s, round_y, round_x] + rounds_z:
+    vector_step(4)
+    for c in [send_a, send_c, send_gl, part_b] + late + last:
         c.wait_send()
 
 
@@ -1273,8 +1360,12 @@
         pltpu.VMEM((rows, features), BF),
         pltpu.VMEM((rows, features), BF),
         pltpu.VMEM((16, features), F32),
-        pltpu.VMEM((3, 16, features), F32),
-        pltpu.VMEM((nz + 2, 16, features), F32),
+        pltpu.VMEM((8, 2, features), F32),
+        pltpu.VMEM((8, 2, features), F32),
+        pltpu.VMEM((nz, 2, features), F32),
+        pltpu.VMEM((8, 2, features), F32),
+        pltpu.VMEM((8, 2, features), F32),
+        pltpu.VMEM((nz, 2, features), F32),
         pltpu.VMEM((HEAD_DIM, length), F32),
         pltpu.VMEM((HEAD_DIM, length), F32),
         pltpu.VMEM((rows, features), BF),
@@ -1290,8 +1381,10 @@
         dma((len(reduces), nz + 2)),
         dma((9,)),
         dma((9,)),
-        dma((nz + 2,)),
-        dma((nz + 2,)),
+        dma((nz + 13,)),
+        dma((nz + 13,)),
+        dma((nz + 6,)),
+        dma((nz + 6,)),
     ]
 
     layer_out, grad_tokens, packed, sums = pl.pallas_call(

time: 148 us -> 146 us (0.986)
  Pallas kernels: 147 us -> 145 us
    pallas_call x1, Pallas kernels: 141 us -> 139 us  [fused_device(): pl.pallas_call(functools.partial(fused_body, nz, rows, features, shard, P...]
where the time goes in v3:
time: 146 us
  Pallas kernels  145 us (99%)
    pallas_call x1, Pallas kernels, fused_device(): pl.pallas_call(functools.partial(fused_body, nz, rows, features, shard, P...  139 us
    pallas_call x1, Pallas kernels, fused_device(): pl.pallas_call(functools.partial(spread_body, width), grid=(steps,), out_...  6.06 us

profile of v3, /device:TPU:0, one launch (start us, length us, event | category | flops | bytes accessed | tf_op | source)
XLA Modules:
  0.0 145.7 jit_solution(6738565522112860614)
XLA Ops:
  0.7 138.8 %shard_map.306 = (bf16[512,768]{1,0:T(8,128)(2,1)}, f32[512,768]{1,0:T(8,128)}, f32[3,96,768]{2,1,0:T(8,128)}, f32[16,768]{1,0:T(8,128)}) custom-call(bf16[512,768]{1,0:T(8,128)(2,1)} %tokens_hbm.1, bf16[512,768]{1,0:T(8,128)(2,1)} %cotangent.1, bf16[4,512,768]{2,1,0:T(8,128)(2,1)} %stack.1, bf16[96,192]{1,0:T(8,128)(2,1)} %w_query.1, ...), custom_call_target="tpu_custom_call" | custom-call | tf_op jit(solution)/shard_map/pallas_call | solution.py:1390
  139.5 6.1 %shard_map.307 = (bf16[512,768]{1,0:T(8,128)(2,1)}, f32[512,768]{1,0:T(8,128)}, f32[4,512,768]{2,1,0:T(8,128)}, f32[96,192]{1,0:T(8,128)}, f32[96,192]{1,0:T(8,1...) custom-call(bf16[512,768]{1,0:T(8,128)(2,1)} %cotangent.1, ...), custom_call_target="tpu_custom_call" | custom-call | tf_op jit(solution)/shard_map/pallas_call | solution.py:1439

commit v4 on v3

--- a/solution.py
+++ b/solution.py
@@ -313,97 +313,96 @@
         ("A", 0, 384, 128),
         ("A", 0, 512, 128),
         ("B", 0, 640, 128),
-        ("A", 1, 0, 256),
-        ("A", 1, 256, 256),
-        ("B", 1, 512, 128),
+        ("A", 1, 0, 128),
+        ("B", 1, 128, 128),
+        ("A", 1, 256, 128),
+        ("A", 1, 384, 256),
         ("B", 1, 640, 128),
-        ("A", 2, 0, 256),
-        ("B", 2, 256, 128),
+        ("A", 2, 0, 128),
+        ("B", 2, 128, 128),
+        ("A", 2, 256, 128),
         ("A", 2, 384, 128),
         ("B", 2, 512, 128),
         ("B", 2, 640, 128),
     ),
     (
-        ("A", 2, 0, 256),
-        ("B", 2, 256, 128),
-        ("A", 2, 384, 256),
-        ("B", 2, 640, 128),
+        ("A", 2, 0, 128),
+        ("B", 2, 128, 256),
+        ("A", 2, 384, 128),
+        ("A", 2, 512, 256),
         ("B", 1, 0, 128),
-        ("A", 1, 128, 128),
+        ("B", 1, 128, 128),
         ("B", 1, 256, 128),
-        ("A", 1, 384, 256),
-        ("B", 1, 640, 128),
-        ("A", 0, 0, 128),
-        ("A", 0, 128, 128),
+        ("A", 1, 384, 128),
+        ("A", 1, 512, 256),
+        ("A", 0, 0, 256),
         ("A", 0, 256, 128),
         ("A", 0, 384, 128),
         ("A", 0, 512, 128),
         ("B", 0, 640, 128),
     ),
     {
-        "norm": ((1, 0, 0), (1, 5, 0), (1, 8, 0), (1, 9, 0),),
-        "mask0": ((1, 1, 0), (1, 11, 0), (1, 13, 0), (1, 14, 0),),
+        "norm": ((1, 0, 0), (1, 5, 0), (1, 7, 0), (1, 10, 0),),
+        "mask0": ((1, 1, 0), (1, 12, 0), (1, 15, 0), (1, 16, 0),),
         "mask2": ((1, 2, 0),),
         "mask3": ((1, 0, 1),),
         "stack2": ((1, 3, 0),),
         "stack3": ((1, 1, 1),),
-        "proj0.0": ((1, 4, 0), (1, 0, 2), (1, 2, 1), (1, 5, 1), (1, 1, 2), (1, 3, 1), (1, 4, 1), (1, 0, 3), (1, 6, 0), (1, 2, 2), (1, 5, 2), (1, 1, 3), (1, 7, 0), (1, 3, 2), (1, 6, 1), (1, 2, 3), (1, 8, 1), (1, 5, 3), (1, 4, 2),),
-        "att0.0": ((1, 7, 1),),
+        "proj0.0": ((1, 4, 0), (1, 0, 2), (1, 2, 1), (1, 5, 1), (1, 1, 2), (1, 3, 1), (1, 4, 1), (1, 0, 3), (1, 6, 0), (1, 2, 2), (1, 7, 1), (1, 5, 2), (1, 1, 3), (1, 3, 2), (1, 6, 1), (1, 8, 0), (1, 2, 3), (1, 9, 0), (1, 5, 3), (1, 4, 2),),
+        "proj0.1": ((1, 7, 2),),
         "att0.1": ((1, 3, 3),),
-        "att0.2": ((1, 9, 1),),
-        "att0.3": ((1, 6, 2),),
-        "att2.0": ((1, 8, 2),),
-        "att2.2": ((1, 4, 3), (1, 10, 0),),
-        "att3.0": ((1, 9, 2),),
-        "att3.2": ((1, 11, 1),),
-        "att3.3": ((1, 7, 2), (1, 8, 3),),
-        "att5.0": ((1, 10, 1),),
-        "att5.2": ((1, 6, 3), (1, 12, 0),),
-        "r.other": ((1, 9, 3),),
-        "r.low": ((1, 13, 1),),
-        "ln2": ((1, 11, 2),),
-        "in0": ((1, 10, 2), (1, 14, 1),),
-        "in1": ((1, 12, 1), (1, 7, 3),),
-        "in3": ((1, 11, 3), (1, 13, 2),),
-        "dc2": ((1, 14, 2),),
-        "dc3": ((1, 12, 2),),
-        "bh0": ((1, 13, 3), (1, 10, 3), (0, 1, 0), (0, 0, 0), (1, 14, 3),),
-        "bh1": ((1, 12, 3), (0, 3, 0),),
-        "bh2": ((0, 1, 1),),
-        "bh3": ((0, 2, 0),),
-        "lnb2": ((0, 0, 1), (0, 3, 1),),
-        "db3": ((0, 1, 2),),
-        "go": ((0, 4, 0), (0, 5, 0),),
-        "dwo": ((0, 0, 2),),
-        "ab0.0": ((0, 1, 3), (0, 2, 1),),
-        "ab0.1": ((0, 3, 2),),
-        "ab0.2": ((0, 7, 0),),
+        "att0.2": ((1, 10, 1),),
+        "att0.3": ((1, 6, 2), (1, 8, 1),),
+        "att2.0": ((1, 9, 1),),
+        "att2.2": ((1, 4, 3), (1, 7, 3), (1, 11, 0),),
+        "proj1.1": ((1, 8, 2), (1, 12, 1),),
+        "att3.0": ((1, 10, 2), (1, 6, 3),),
+        "att4.1": ((1, 9, 2), (1, 13, 0),),
+        "att4.3": ((1, 11, 1),),
+        "att5.2": ((1, 8, 3), (1, 14, 0),),
+        "wo": ((1, 12, 2),),
+        "r.other": ((1, 10, 3),),
+        "r.low": ((1, 15, 1),),
+        "in0": ((1, 11, 2), (1, 13, 1), (1, 16, 1),),
+        "in1": ((1, 9, 3), (1, 12, 3), (1, 14, 1),),
+        "in3": ((1, 15, 2),),
+        "dc0": ((1, 13, 2),),
+        "dc1": ((1, 11, 3),),
+        "dc3": ((1, 14, 2), (1, 16, 2),),
+        "bh0": ((1, 15, 3), (1, 13, 3), (0, 1, 0), (0, 0, 0), (1, 16, 3),),
+        "bh1": ((1, 14, 3),),
+        "bi0": ((0, 2, 0),),
+        "bh3": ((0, 0, 1), (0, 3, 0),),
+        "lnb2": ((0, 1, 1), (0, 2, 1),),
+        "go": ((0, 4, 0), (0, 7, 0),),
+        "ab0.0": ((0, 0, 2),),
+        "ab0.1": ((0, 3, 1), (0, 8, 0),),
+        "ab0.2": ((0, 2, 2),),
         "ab1.0": ((0, 4, 1),),
-        "ab1.1": ((0, 3, 3), (0, 0, 3), (0, 5, 1),),
-        "ab1.3": ((0, 6, 0),),
-        "ab2.0": ((0, 2, 2),),
-        "ab2.3": ((0, 4, 2),),
-        "da0": ((0, 5, 2), (0, 8, 0),),
-        "ab3.0": ((0, 9, 0),),
-        "ab3.1": ((0, 4, 3), (0, 6, 1),),
-        "ab3.2": ((0, 2, 3), (0, 7, 1),),
-        "ab3.3": ((0, 10, 0),),
-        "ab4.0": ((0, 5, 3),),
-        "ab4.2": ((0, 8, 1),),
-        "ab4.3": ((0, 14, 0),),
-        "ab5.0": ((0, 6, 2), (0, 11, 0),),
-        "ab5.3": ((0, 7, 2),),
-        "da2": ((0, 6, 3),),
-        "da3": ((0, 8, 2),),
-        "bp0": ((0, 9, 1), (0, 12, 0),),
-        "bp1": ((0, 10, 1), (0, 14, 1),),
-        "lnb1": ((0, 7, 3), (0, 8, 3), (0, 9, 2), (0, 11, 1), (0, 13, 0),),
-        "vs0": ((0, 10, 2), (0, 12, 1), (0, 14, 2),),
-        "vs1": ((0, 9, 3), (0, 11, 2), (0, 13, 1),),
-        "out1": ((0, 10, 3), (0, 12, 2), (0, 14, 3),),
-        "fin": ((0, 11, 3), (0, 13, 2),),
-        "vs2": ((0, 12, 3),),
-        "end": ((0, 13, 3),),
+        "ab1.1": ((0, 0, 3), (0, 5, 0),),
+        "ab2.0": ((0, 2, 3),),
+        "ab2.1": ((0, 3, 2),),
+        "ab2.2": ((0, 6, 0),),
+        "ab2.3": ((0, 1, 2),),
+        "da0": ((0, 4, 2),),
+        "da1": ((0, 5, 1),),
+        "ab3.0": ((0, 9, 0), (0, 7, 1),),
+        "ab3.1": ((0, 1, 3),),
+        "ab3.2": ((0, 4, 3),),
+        "ab3.3": ((0, 3, 3), (0, 8, 1), (0, 6, 1),),
+        "ab4.3": ((0, 13, 0),),
+        "ab5.0": ((0, 5, 2), (0, 7, 2), (0, 10, 0),),
+        "ab5.3": ((0, 8, 2),),
+        "da2": ((0, 5, 3),),
+        "da3": ((0, 6, 2), (0, 11, 0),),
+        "bp0": ((0, 7, 3), (0, 9, 1),),
+        "bp1": ((0, 13, 1),),
+        "lnb1": ((0, 6, 3), (0, 8, 3), (0, 10, 1), (0, 12, 0),),
+        "vs0": ((0, 9, 2), (0, 11, 1), (0, 13, 2),),
+        "vs1": ((0, 10, 2), (0, 12, 1), (0, 13, 3),),
+        "out1": ((0, 11, 2),),
+        "fin": ((0, 9, 3), (0, 10, 3), (0, 12, 2),),
+        "end": ((0, 11, 3), (0, 12, 3),),
     },
 )
 

time: 146 us -> 147 us (level)
  no operation moved by 1% of the time
where the time goes in v4:
time: 147 us
  Pallas kernels  146 us (99%)
    pallas_call x1, Pallas kernels, fused_device(): pl.pallas_call(functools.partial(fused_body, nz, rows, features, shard, P...  140 us
    pallas_call x1, Pallas kernels, fused_device(): pl.pallas_call(functools.partial(spread_body, width), grid=(steps,), out_...  6.06 us

profile of v4, /device:TPU:0, one launch (start us, length us, event | category | flops | bytes accessed | tf_op | source)
XLA Modules:
  0.0 146.8 jit_solution(4823639658336879029)
XLA Ops:
  0.7 139.9 %shard_map.306 = (bf16[512,768]{1,0:T(8,128)(2,1)}, f32[512,768]{1,0:T(8,128)}, f32[3,96,768]{2,1,0:T(8,128)}, f32[16,768]{1,0:T(8,128)}) custom-call(bf16[512,768]{1,0:T(8,128)(2,1)} %tokens_hbm.1, bf16[512,768]{1,0:T(8,128)(2,1)} %cotangent.1, bf16[4,512,768]{2,1,0:T(8,128)(2,1)} %stack.1, bf16[96,192]{1,0:T(8,128)(2,1)} %w_query.1, ...), custom_call_target="tpu_custom_call" | custom-call | tf_op jit(solution)/shard_map/pallas_call | solution.py:1389
  140.5 6.1 %shard_map.307 = (bf16[512,768]{1,0:T(8,128)(2,1)}, f32[512,768]{1,0:T(8,128)}, f32[4,512,768]{2,1,0:T(8,128)}, f32[96,192]{1,0:T(8,128)}, f32[96,192]{1,0:T(8,1...) custom-call(bf16[512,768]{1,0:T(8,128)(2,1)} %cotangent.1, ...), custom_call_target="tpu_custom_call" | custom-call | tf_op jit(solution)/shard_map/pallas_call | solution.py:1438
